TPU v7x, 512 devices: a whole 4x8x8 slice. The times are simulated.
512 devices in a mesh: section: 8 (over z), slab: 64 (over x, y, core).
Axes of the slice: x: 4, y: 8, z: 8, core: 2. Of those that a mesh axis runs over, the one named last changes fastest.
Arguments:
- fields: bfloat16 [8, 4, 128, 128, 128], P('section', None, 'slab'), may hold values from -6 to 6
- lift_weight: bfloat16 [4, 32], replicated, may hold values from -3 to 3
- lift_bias: bfloat16 [32], replicated, may hold values from -3 to 3
- spectral_weight: bfloat16 [2, 2, 32, 32, 16384], P(None, None, None, 'section', 'slab'), may hold values from -0.75 to 0.75
- bypass_weight: bfloat16 [2, 32, 32], replicated, may hold values from -1 to 1
- bypass_bias: bfloat16 [2, 32], replicated, may hold values from -3 to 3
Outputs:
- features: bfloat16 [8, 32, 128, 128, 128], P('section', None, 'slab')
All inputs are finite; a program needn't handle non-finite values.
Results may differ from a plain program's by a relative error of at most 0.015.
Values may be sent and summed in bfloat16 or wider, within the bound.
No kernel may reach another device: no remote copies, remote signals or barrier semaphores. Data moves between devices by JAX's collectives and lax.ppermute only.
A program may use at most 64 MiB of HBM per device.

v0:
```python
import math

import jax
import jax.numpy as jnp
import ml_dtypes
import numpy as np
from jax import lax
from jax.experimental import pallas as pl
from jax.experimental.pallas import tpu as pltpu
from jax.sharding import PartitionSpec as P

K = 16
HALF = 2 * K
LENGTH = 128
SLABS = 64
BF = jnp.bfloat16
F32 = jnp.float32


def wave(freqs):
    where = np.arange(LENGTH, dtype=np.int64)[None, :]
    step = (freqs % LENGTH)[:, None] * where % LENGTH
    phase = step.astype(np.float32) * np.float32(2.0 * math.pi / LENGTH)
    cosine = np.cos(phase).astype(ml_dtypes.bfloat16).astype(np.float32)
    sine = np.sin(phase).astype(ml_dtypes.bfloat16).astype(np.float32)
    return cosine, sine


def make_tables():
    base = np.arange(HALF)
    signed = np.where(base < K, base, base - HALF)
    cos, sin = wave(signed)
    cos_z, sin_z = wave(np.arange(K))
    double = np.where(np.arange(K) == 0, 1.0, 2.0)[:, None]
    table = {}
    pair = np.stack([cos, -sin], 0).reshape(2, 2, K, LENGTH)
    for name, many in (("fwd_y8", 8), ("fwd_y4", 4)):
        block = np.einsum("cd,rhpy->cyrhdp", np.eye(many), pair)
        table[name] = block.reshape(many * LENGTH, 4 * many * K)
    table["fwd_x"] = np.concatenate(
        [np.concatenate([cos, sin], 1), np.concatenate([-sin, cos], 1)], 0
    )
    fwd_z = np.stack([np.stack([cos_z, sin_z], 1), np.stack([-sin_z, cos_z], 1)], 0)
    fwd_z = fwd_z.reshape(2, K, 2, SLABS, 2)
    full = np.einsum("gf,akrsz->gaksfrz", np.eye(4), fwd_z)
    table["fwd_z"] = full.reshape(4 * HALF, SLABS * 16)
    table["fwd_z0"] = np.einsum("akrsz->zaksr", fwd_z).reshape(2 * HALF, SLABS * 2)
    cz, sz = cos_z * double * 0.25, sin_z * double * 0.25
    inv_z = np.stack([np.stack([cz, -sz], 0), np.stack([sz, cz], 0)], 0)
    inv_z = inv_z.reshape(2, 2, K, SLABS, 2)
    table["inv_z"] = np.einsum("gf,arksz->sgazfrk", np.eye(4), inv_z).reshape(SLABS * 16, 4 * HALF)
    inv_x = np.stack([np.stack([cos, -sin], 0), np.stack([sin, cos], 0)], 0)
    table["inv_x"] = np.einsum("arpx->axrp", inv_x).reshape(2 * LENGTH, 2 * HALF) * 0.125
    table["inv_y"] = (
        np.einsum("cd,rhpy->rhcpdy", np.eye(8), pair).reshape(512, 8 * LENGTH) * 0.125
    )
    one_x = (cos.sum(1) - 1j * sin.sum(1)) / math.sqrt(LENGTH)
    one_z = (cos_z.sum(1) - 1j * sin_z.sum(1)) / math.sqrt(LENGTH)
    return table, one_x, one_z


def split(value):
    return np.stack([value.real, value.imag], 0).astype(np.float32)


def dot(left, right):
    return jnp.dot(left, right, preferred_element_type=F32)


def nt_dot(left, right):
    return lax.dot_general(left, right, (((1,), (1,)), ((), ())), preferred_element_type=F32)


def spread_kernel(bypass_ref, lift_ref, bypass_bias_ref, lift_bias_ref, kb_ref, kl_ref, bias_ref):
    def picks(rows, cols):
        row = lax.broadcasted_iota(jnp.int32, (rows, cols), 0)
        col = lax.broadcasted_iota(jnp.int32, (rows, cols), 1)
        return row, col

    row, col = picks(512, 32)
    expand = jnp.where(row // 16 == col, 1.0, 0.0).astype(BF)
    row, col = picks(512, 512)
    same = (row % 16) == (col % 16)
    for layer in range(2):
        tall = lax.dot_general(
            expand, bypass_ref[layer], (((1,), (1,)), ((), ())), preferred_element_type=F32
        ).astype(BF)
        wide = nt_dot(tall, expand)
        kb_ref[layer] = jnp.where(same, wide, 0.0).astype(BF)
    row, col = picks(64, 4)
    expand4 = jnp.where(row // 16 == col, 1.0, 0.0).astype(BF)
    tall = lax.dot_general(
        expand, lift_ref[...], (((1,), (1,)), ((), ())), preferred_element_type=F32
    ).astype(BF)
    row, col = picks(512, 64)
    kl_ref[...] = jnp.where((row % 16) == (col % 16), nt_dot(tall, expand4), 0.0).astype(BF)
    ones = jnp.ones((32, LENGTH), BF)
    expand = expand.astype(F32)
    for index in range(3):
        vector = bypass_bias_ref[index : index + 1] if index < 2 else lift_bias_ref[...]
        bias_ref[index] = dot((expand * vector.astype(F32)).astype(BF), ones)


def start_kernel(fields_ref, fwd_y_ref, fwd_x_ref, out_ref, rows):
    lane = lax.broadcasted_iota(jnp.int32, (64, LENGTH), 1)
    made = []
    for z in range(2):
        wide = jnp.concatenate([fields_ref[0, c, z] for c in range(4)], axis=1)
        along = dot(wide, fwd_y_ref[...]).astype(BF)
        stacked = jnp.concatenate([along[:, :128], along[:, 128:]], axis=0)
        made.append(dot(fwd_x_ref[...], stacked) * (1.0 / LENGTH))
    first = jnp.where(lane < 64, made[0], pltpu.roll(made[1], 64, 1))
    second = jnp.where(lane < 64, pltpu.roll(made[0], 64, 1), made[1])
    for h, value in enumerate((first, second)):
        for r in range(2):
            rows[pl.ds(h * 2 + r, 32, stride=4), :] = value[r * 32 : r * 32 + 32]
    out_ref[...] = rows[...].astype(BF)


def mix(weight_ref, modes, pattern, turned, inv_z_ref, out_ref):
    low = lax.broadcasted_iota(jnp.int32, (8, LENGTH), 0) < 4
    for pair in range(16):
        for r in range(2):
            for half in range(2):
                even = jnp.broadcast_to(modes[r, half, 2 * pair : 2 * pair + 1, :], (8, LENGTH))
                odd = jnp.broadcast_to(modes[r, half, 2 * pair + 1 : 2 * pair + 2, :], (8, LENGTH))
                pattern[pair, r, half] = jnp.where(low, even, odd)
    slot = lax.broadcasted_iota(jnp.int32, (8, LENGTH), 1) // K
    mixed = {}
    for g in range(4):
        total = {}
        for side in range(2):
            section = 2 * g + side
            acc = [[jnp.zeros((8, LENGTH), F32) for _ in range(2)] for _ in range(2)]
            for quad in range(8):
                real = weight_ref[section, 0, quad * 16 : quad * 16 + 16, :].astype(F32)
                imag = weight_ref[section, 1, quad * 16 : quad * 16 + 16, :].astype(F32)
                for sub in range(2):
                    pair = quad * 2 + sub
                    for half in range(2):
                        wr = real[sub * 8 : sub * 8 + 8, half * 128 : half * 128 + 128]
                        wi = imag[sub * 8 : sub * 8 + 8, half * 128 : half * 128 + 128]
                        mr, mi = pattern[pair, 0, half], pattern[pair, 1, half]
                        acc[0][half] = acc[0][half] + wr * mr - wi * mi
                        acc[1][half] = acc[1][half] + wr * mi + wi * mr
            for r in range(2):
                for half in range(2):
                    value = acc[r][half]
                    total[side, r, half] = value + pltpu.roll(value, 4, 0)
        for r in range(2):
            for half in range(2):
                mixed[g, r, half] = jnp.where(low, total[0, r, half], total[1, r, half])
    for py in range(K):
        half, at = py // 8, py % 8
        value = None
        for g in range(4):
            for r in range(2):
                where = 2 * g + r
                moved = mixed[g, r, half]
                if where != at:
                    moved = pltpu.roll(moved, (where - at) * K % LENGTH, 1)
                value = moved if value is None else jnp.where(slot == where, moved, value)
        turned[pl.ds(py, 8, stride=K), :] = value
    out_ref[...] = nt_dot(inv_z_ref[...], turned[...].astype(BF)).astype(BF)


def unravel(turned, groups, modes):
    slot = lax.broadcasted_iota(jnp.int32, (8, LENGTH), 1) // K
    parts = [turned[pl.ds(py, 8, stride=K), :] for py in range(K)]
    for g in range(groups):
        for r in range(2):
            source = 2 * g + r
            for half in range(2):
                value = None
                for at in range(8):
                    moved = parts[half * 8 + at]
                    if at != source:
                        moved = pltpu.roll(moved, (at - source) * K % LENGTH, 1)
                    value = moved if value is None else jnp.where(slot == at, moved, value)
                modes[r, half, g * 8 : g * 8 + 8, :] = value


def dropped(place_ref, shape):
    row = lax.broadcasted_iota(jnp.int32, shape, 0)
    lane = lax.broadcasted_iota(jnp.int32, shape, 1)
    origin = jnp.logical_and(row % K == 0, lane % K == 0)
    return jnp.logical_and(origin, place_ref[0] == 0)


def first_mix_kernel(
    place_ref, one_x_ref, got_ref, weight_ref, lift_ref, one_y_ref, one_z_ref, fwd_z_ref,
    inv_z_ref, out_ref, turned, small, modes, pattern,
):
    both = dot(fwd_z_ref[...], got_ref[...])
    lane = lax.broadcasted_iota(jnp.int32, (HALF, LENGTH), 1)
    value = both[:HALF] + pltpu.roll(both[HALF:], 64, 1)
    value = jnp.where(lane < 64, value, 0.0) * (1.0 / math.sqrt(LENGTH))
    place = place_ref[0]
    xr, xi = one_x_ref[0, place // 2], one_x_ref[1, place // 2]
    yr = jnp.where(place % 2 == 0, one_y_ref[0, 0:1, :], one_y_ref[1, 0:1, :])
    yi = jnp.where(place % 2 == 0, one_y_ref[0, 1:2, :], one_y_ref[1, 1:2, :])
    pr, pi = xr * yr - xi * yi, xr * yi + xi * yr
    zr, zi = one_z_ref[0], one_z_ref[1]
    ones = jnp.concatenate([zr * pr - zi * pi, zr * pi + zi * pr], axis=0)
    value = jnp.where(lane // K == 4, ones, value)
    value = jnp.where(dropped(place_ref, value.shape), 0.0, value)
    value = jnp.concatenate([value, jnp.zeros((LENGTH - HALF, LENGTH), F32)], axis=0)
    turned[...] = value.T
    unravel(turned, 1, small)
    for r in range(2):
        for half in range(2):
            total = jnp.zeros((32, LENGTH), F32)
            for c in range(5):
                total = total + lift_ref[:, c : c + 1] * small[r, half, c : c + 1, :]
            modes[r, half] = total
    mix(weight_ref, modes, pattern, turned, inv_z_ref, out_ref)


def mix_kernel(place_ref, got_ref, weight_ref, fwd_z_ref, inv_z_ref, out_ref, turned, modes, pattern):
    value = dot(fwd_z_ref[...], got_ref[...]) * (1.0 / math.sqrt(LENGTH))
    value = jnp.where(dropped(place_ref, value.shape), 0.0, value)
    turned[...] = value.T
    unravel(turned, 4, modes)
    mix(weight_ref, modes, pattern, turned, inv_z_ref, out_ref)


def inverse(got_ref, inv_x_ref, inv_y_ref, rows, field):
    rows[...] = got_ref[...].astype(F32)
    for g in range(4):
        for z in range(2):
            parts = []
            for h in range(2):
                pieces = [
                    rows[pl.ds(h * 16 + g * 4 + r * 2 + z, 32, stride=32), :] for r in range(2)
                ]
                parts.append(jnp.concatenate(pieces, axis=0).astype(BF))
            along = dot(inv_x_ref[...], jnp.concatenate(parts, axis=1)).astype(BF)
            wide = jnp.concatenate([along[:128], along[128:]], axis=1)
            made = dot(wide, inv_y_ref[...])
            for o in range(8):
                field[g * 8 + o, z] = made[:, o * 128 : o * 128 + 128]


def activate(value):
    inner = value * (0.7978845608028654 + 0.035677408136300125 * value * value)
    half = 0.5 * value
    return half + half * jnp.tanh(inner)


def pointwise(block, hidden, kb_ref, bias, field):
    bypassed = dot(kb_ref[...], hidden)
    made = []
    for z in range(2):
        part = field[:, z, block * 16 : block * 16 + 16, :].reshape(512, LENGTH)
        value = bypassed[:, z * 128 : z * 128 + 128] + bias + part
        made.append(activate(value).astype(BF))
    return made


def middle_kernel(
    got_ref, fields_ref, kl_ref, kb_ref, bias_ref, inv_x_ref, inv_y_ref, fwd_y_ref, fwd_x_ref,
    hidden_ref, out_ref, rows, field,
):
    inverse(got_ref, inv_x_ref, inv_y_ref, rows, field)
    lift_bias = bias_ref[2]
    lift_bias = jnp.concatenate([lift_bias, lift_bias], axis=1)
    for block in range(8):
        span = slice(block * 16, block * 16 + 16)
        raw = [fields_ref[0, :, z, span, :].reshape(64, LENGTH) for z in range(2)]
        hidden = (dot(kl_ref[...], jnp.concatenate(raw, axis=1)) + lift_bias).astype(BF)
        made = pointwise(block, hidden, kb_ref.at[0], bias_ref[0], field)
        for z in range(2):
            hidden_ref[:, z, span, :] = made[z].reshape(32, 16, LENGTH)
    for g in range(4):
        for z in range(2):
            wide = jnp.concatenate([hidden_ref[g * 8 + c, z] for c in range(8)], axis=1)
            along = dot(wide, fwd_y_ref[...]).astype(BF)
            stacked = jnp.concatenate([along[:, :256], along[:, 256:]], axis=0)
            spectrum = dot(fwd_x_ref[...], stacked) * (1.0 / LENGTH)
            for h in range(2):
                for r in range(2):
                    at = h * 16 + g * 4 + r * 2 + z
                    rows[pl.ds(at, 32, stride=32), :] = spectrum[
                        r * 32 : r * 32 + 32, h * 128 : h * 128 + 128
                    ]
    out_ref[...] = rows[...].astype(BF)


def last_kernel(
    got_ref, hidden_ref, kb_ref, bias_ref, inv_x_ref, inv_y_ref, out_ref, rows, field
):
    inverse(got_ref, inv_x_ref, inv_y_ref, rows, field)
    for block in range(8):
        span = slice(block * 16, block * 16 + 16)
        raw = [hidden_ref[:, z, span, :].reshape(512, LENGTH) for z in range(2)]
        made = pointwise(block, jnp.concatenate(raw, axis=1), kb_ref.at[1], bias_ref[1], field)
        for z in range(2):
            out_ref[0, :, z, span, :] = made[z].reshape(32, 16, LENGTH)


def vmem(count):
    return [pl.BlockSpec(memory_space=pltpu.VMEM)] * count


def call(kernel, name, inputs, outputs, scratch, scalars=0):
    return pl.pallas_call(
        kernel,
        name=name,
        out_shape=outputs,
        in_specs=[pl.BlockSpec(memory_space=pltpu.SMEM)] * scalars + vmem(inputs),
        out_specs=vmem(len(outputs)),
        scratch_shapes=[pltpu.VMEM(shape, F32) for shape in scratch],
        compiler_params=pltpu.CompilerParams(vmem_limit_bytes=40 << 20),
    )


def exchange(value):
    return lax.all_to_all(value, "slab", split_axis=0, concat_axis=0, tiled=True)


def solution(mesh):
    table, one_x, one_z = make_tables()
    const = {name: value.astype(ml_dtypes.bfloat16) for name, value in table.items()}
    ones_x = split(one_x)
    ones_y = np.tile(split(one_x).reshape(2, 2, 1, K), (1, 1, 8, 1)).reshape(2, 2, LENGTH)
    ones_y = ones_y.transpose(1, 0, 2)
    ones_z = np.repeat(split(one_z)[:, :, None], LENGTH, axis=2)

    def on_device(fields, lift_weight, lift_bias, spectral_weight, bypass_weight, bypass_bias):
        place = lax.axis_index("slab").reshape(1)
        gathered = []
        for layer in range(2):
            local = spectral_weight[layer].reshape(2, LENGTH, 256)
            gathered.append(lax.all_gather(local, "section", axis=0))
        lifting = jnp.concatenate([lift_weight, lift_bias[None]], axis=0).T.astype(F32)
        (spectrum,) = call(
            start_kernel, "start", 3, [jax.ShapeDtypeStruct((128, 128), BF)], [(128, 128)]
        )(fields, const["fwd_y4"], const["fwd_x"])
        kb, kl, bias = call(
            spread_kernel,
            "spread",
            4,
            [
                jax.ShapeDtypeStruct((2, 512, 512), BF),
                jax.ShapeDtypeStruct((512, 64), BF),
                jax.ShapeDtypeStruct((3, 512, LENGTH), F32),
            ],
            [],
        )(bypass_weight, lift_weight, bypass_bias, lift_bias[None])
        packed = jax.ShapeDtypeStruct((1024, LENGTH), BF)
        square, modes, pattern = (128, 128), (2, 2, 32, 128), (16, 2, 2, 8, 128)
        (planes,) = call(
            first_mix_kernel,
            "mix0",
            7,
            [packed],
            [square, (2, 2, 8, 128), modes, pattern],
            scalars=2,
        )(
            place, ones_x, exchange(spectrum), gathered[0], lifting, ones_y, ones_z,
            const["fwd_z0"], const["inv_z"],
        )
        hidden, spectrum = call(
            middle_kernel,
            "middle",
            9,
            [jax.ShapeDtypeStruct((32, 2, 128, 128), BF), packed],
            [(1024, 128), (32, 2, 128, 128)],
        )(
            exchange(planes), fields, kl, kb, bias, const["inv_x"], const["inv_y"],
            const["fwd_y8"], const["fwd_x"],
        )
        (planes,) = call(
            mix_kernel, "mix1", 4, [packed], [square, modes, pattern], scalars=1
        )(place, exchange(spectrum), gathered[1], const["fwd_z"], const["inv_z"])
        (features,) = call(
            last_kernel,
            "last",
            6,
            [jax.ShapeDtypeStruct((1, 32, 2, 128, 128), BF)],
            [(1024, 128), (32, 2, 128, 128)],
        )(exchange(planes), hidden, kb, bias, const["inv_x"], const["inv_y"])
        return features

    placed = (
        P("section", None, "slab", None, None),
        P(),
        P(),
        P(None, None, None, "section", "slab"),
        P(),
        P(),
    )
    return jax.shard_map(
        on_device,
        mesh=mesh,
        in_specs=placed,
        out_specs=P("section", None, "slab", None, None),
        check_vma=False,
    )
```

profile of v0, /device:TPU:1, one launch (start us, length us, event | category | flops | bytes accessed | tf_op | source)
XLA Modules:
  0.0 151.7 jit_solution(16874514750189992838)
XLA Ops:
  6.5 0.0 all-gather.3.cloned.1.call-start
  6.5 1.2 fusion
  7.7 0.7 all_gather_reshape_squeeze.6
  8.4 0.0 all-gather.3.cloned.1.call-update
  8.4 0.0 all-gather.5.cloned.1.call-start
  8.5 0.7 all_gather_reshape_squeeze.7
  9.2 0.0 all-gather.5.cloned.1.call-update
  9.2 0.0 copy-start.4
  9.2 0.9 copy-done.4
  10.1 0.9 copy-done.12
  11.1 0.8 copy-done.14
  11.9 0.0 copy-start.10
  11.9 1.3 start.1
  13.1 11.6 %all-to-all-start = ((bf16[64,2,128]{2,1,0:T(2,128)(2,1)}), bf16[64,2,128]{2,1,0:T(2,128)(2,1)S(1)}, u32[]{:S(2)}, u32[]{:S(2)}) async-start(bf16[64,2,128]{2,1,0:T(2,128)(2,1)} %bitcast.1), calls=%async_computation | async-start | bytes 65536 | tf_op jit(solution)/shard_map/all_to_all | solution.py:318
  24.8 0.7 maximum_convert_fusion
  25.5 0.1 copy.21
  25.6 8.5 %all-to-all-done = bf16[64,2,128]{2,1,0:T(2,128)(2,1)S(1)} async-done(((bf16[64,2,128]{2,1,0:T(2,128)(2,1)}), bf16[64,2,128]{2,1,0:T(2,128)(2,1)S(1)}, u32[]{:S(2)}, u32[]{:S(2)}) %all-to-all-start) | async-done | bytes 32800 | tf_op jit(solution)/shard_map/all_to_all | solution.py:318
  34.0 18.6 %all-gather.3.cloned.1.call-done.weight_ref = bf16[8,2,128,256]{3,2,1,0:T(8,128)(2,1)} async-done(((bf16[1,2,128,256]{3,2,1,0:T(8,128)(2,1)}), bf16[8,2,128,256]{3,2,1,0:T(8,128)(2,1)}) %all-gather.3.cloned.1.call-update) | async-done | bytes 1048592 | tf_op jit(solution)/shard_map/all_gather | solution.py:334
  52.7 1.2 copy-done.6
  53.9 0.9 copy-done.7
  54.9 0.7 copy-done.18
  55.6 0.7 copy-done.19
  56.3 0.7 copy-done.22
  57.0 0.7 copy-done.24
  57.7 2.5 %mix0.1 = bf16[1024,128]{1,0:T(8,128)(2,1)} custom-call(s32[1]{0:T(128)} %bitcast.place_ref, f32[2,32]{1,0:T(2,128)S(1)} %copy-done.24, bf16[128,128]{1,0:T(8,128)(2,1)S(1)} %bitcast.16, bf16[8,2,128,256]{3,2,1,0:T(8,128)(2,1)S(1)} %copy-done.6, f32[32,5]{1,0:T(8,128)S(1)} %bitcast.17, f32[2,2,128]{2,1,0:T(2,128)S(1)} %copy-done.22, ...), custom_call_target="tpu_custom_call" | custom-call | tf_op jit(solution)/shard_map/mix0/pallas_call | solution.py:352
  60.1 14.8 %all-to-all-start.1 = ((bf16[64,16,128]{2,1,0:T(8,128)(2,1)}), bf16[64,16,128]{2,1,0:T(8,128)(2,1)S(1)}, u32[]{:S(2)}, u32[]{:S(2)}) async-start(bf16[64,16,128]{2,1,0:T(8,128)(2,1)} %bitcast.5), calls=%async_computation.1 | async-start | bytes 524288 | tf_op jit(solution)/shard_map/all_to_all | solution.py:318
  75.0 0.0 copy-done.20
  75.0 0.9 spread.1
  76.0 0.7 copy-done.16
  76.6 10.4 %all-to-all-done.1 = bf16[64,16,128]{2,1,0:T(8,128)(2,1)S(1)} async-done(((bf16[64,16,128]{2,1,0:T(8,128)(2,1)}), bf16[64,16,128]{2,1,0:T(8,128)(2,1)S(1)}, u32[]{:S(2)}, u32[]{:S(2)}) %all-to-all-start.1) | async-done | bytes 262176 | tf_op jit(solution)/shard_map/all_to_all | solution.py:318
  87.0 0.0 copy-done.5
  87.0 0.0 copy-done.10
  87.0 0.0 copy-start.9
  87.0 1.2 copy-done.9
  88.2 0.9 copy-done.17
  89.2 7.5 %middle.1 = (bf16[32,2,128,128]{3,2,1,0:T(8,128)(2,1)S(1)}, bf16[1024,128]{1,0:T(8,128)(2,1)S(1)}) custom-call(bf16[1024,128]{1,0:T(8,128)(2,1)S(1)} %bitcast.11, bf16[1,4,2,128,128]{4,3,2,1,0:T(8,128)(2,1)S(1)} %copy-done.5, bf16[512,64]{1,0:T(8,128)(2,1)S(1)} %copy-done.17, bf16[2,512,512]{2,1,0:T(8,128)(2,1)S(1)} %get-tuple-element.11.kb_ref, ...), custom_call_target="tpu_custom_call" | custom-call | tf_op jit(solution)/shard_map/middle/pallas_call | solution.py:363
  96.7 0.0 copy-start.1
  96.7 1.3 copy-done.1
  98.0 0.7 copy-done.13
  98.7 6.0 %all-to-all-start.2 = ((bf16[64,16,128]{2,1,0:T(8,128)(2,1)}), bf16[64,16,128]{2,1,0:T(8,128)(2,1)S(1)}, u32[]{:S(2)}, u32[]{:S(2)}) async-start(bf16[64,16,128]{2,1,0:T(8,128)(2,1)} %bitcast.15), calls=%async_computation.2 | async-start | bytes 524288 | tf_op jit(solution)/shard_map/all_to_all | solution.py:318
  104.8 0.0 all-gather.5.cloned.1.call-done.weight_ref
  104.8 12.0 %all-to-all-done.2 = bf16[64,16,128]{2,1,0:T(8,128)(2,1)S(1)} async-done(((bf16[64,16,128]{2,1,0:T(8,128)(2,1)}), bf16[64,16,128]{2,1,0:T(8,128)(2,1)S(1)}, u32[]{:S(2)}, u32[]{:S(2)}) %all-to-all-start.2) | async-done | bytes 262176 | tf_op jit(solution)/shard_map/all_to_all | solution.py:318
  116.8 1.4 copy-done.3
  118.1 0.9 copy-done.8
  119.1 0.9 copy-done.11
  120.0 1.2 mix1.1
  121.2 17.8 %all_to_all.44 = bf16[64,16,128]{2,1,0:T(8,128)(2,1)S(1)} all-to-all(bf16[64,16,128]{2,1,0:T(8,128)(2,1)S(1)} %bitcast.14), channel_id=1, replica_groups=mesh['section'=8,'slab'=64] {'slab'}, dimensions={0} | all-to-all | bytes 524288 | tf_op jit(solution)/shard_map/all_to_all | solution.py:318
  139.1 5.8 %last.1 = bf16[1,32,2,128,128]{4,3,2,1,0:T(8,128)(2,1)} custom-call(bf16[1024,128]{1,0:T(8,128)(2,1)S(1)} %bitcast.13, bf16[32,2,128,128]{3,2,1,0:T(8,128)(2,1)S(1)} %copy-done.2, bf16[2,512,512]{2,1,0:T(8,128)(2,1)S(1)} %get-tuple-element.11.kb_ref, f32[3,512,128]{2,1,0:T(8,128)S(1)} %get-tuple-element.12.bias_ref, bf16[256,64]{1,0:T(8,128)(2,1)S(1)} %copy-done.10, ...), custom_call_target="tpu_custom_call" | custom-call | tf_op jit(solution)/shard_map/last/pallas_call | solution.py:376
  (28 shorter events, 0.0 us)
Async XLA Ops:
  6.5 80.5 %copy-start.15 = (bf16[64,256]{1,0:T(8,128)(2,1)S(1)}, bf16[64,256]{1,0:T(8,128)(2,1)}, u32[]{:S(2)}) copy-start(bf16[64,256]{1,0:T(8,128)(2,1)} %constant.27.clone.fwd_x_ref) | copy-start | bytes 98308
  6.5 80.5 %copy-start = (bf16[512,1024]{1,0:T(8,128)(2,1)S(1)}, bf16[512,1024]{1,0:T(8,128)(2,1)}, u32[]{:S(2)}) copy-start(bf16[512,1024]{1,0:T(8,128)(2,1)} %constant.34.clone.inv_y_ref) | copy-start | bytes 3145732
  6.5 80.5 %copy-start.5 = (bf16[1,4,2,128,128]{4,3,2,1,0:T(8,128)(2,1)S(1)}, bf16[1,4,2,128,128]{4,3,2,1,0:T(8,128)(2,1)}, u32[]{:S(2)}) copy-start(bf16[1,4,2,128,128]{4,3,2,1,0:T(8,128)(2,1)} %fields_ref.3) | copy-start | bytes 786436
  6.5 46.1 %all-gather.3.cloned.1.call-start = ((), (), s32[]{:S(2)}) async-start(), calls=%async_computation.4 | async-start | bytes 1179648 | tf_op jit(solution)/shard_map/all_gather | solution.py:334
  8.4 96.4 %all-gather.5.cloned.1.call-start = ((), (), s32[]{:S(2)}) async-start(), calls=%async_computation.5 | async-start | bytes 1179648 | tf_op jit(solution)/shard_map/all_gather | solution.py:334
  9.2 1.0 copy-start.4
  10.1 0.9 copy-start.12
  11.1 0.8 copy-start.14
  11.8 63.1 %copy-start.20 = (bf16[2,32,32]{2,1,0:T(8,128)(2,1)S(1)}, bf16[2,32,32]{2,1,0:T(8,128)(2,1)}, u32[]{:S(2)}) copy-start(bf16[2,32,32]{2,1,0:T(8,128)(2,1)} %bypass_ref.1) | copy-start | bytes 12292
  11.9 63.1 %copy-start.21 = (bf16[4,32]{1,0:T(4,128)(2,1)S(1)}, bf16[4,32]{1,0:T(4,128)(2,1)}, u32[]{:S(2)}) copy-start(bf16[4,32]{1,0:T(4,128)(2,1)} %lift_ref.1) | copy-start | bytes 772
  11.9 63.2 %copy-start.23 = (bf16[32]{0:T(256)(128)(2,1)S(1)}, bf16[32]{0:T(256)(128)(2,1)}, u32[]{:S(2)}) copy-start(bf16[32]{0:T(256)(128)(2,1)} %param.19) | copy-start | bytes 196
  11.9 63.2 %copy-start.25 = (bf16[2,32]{1,0:T(2,128)(2,1)S(1)}, bf16[2,32]{1,0:T(2,128)(2,1)}, u32[]{:S(2)}) copy-start(bf16[2,32]{1,0:T(2,128)(2,1)} %bypass_bias_ref.1) | copy-start | bytes 388
  11.9 75.1 %copy-start.10 = (bf16[256,64]{1,0:T(8,128)(2,1)S(1)}, bf16[256,64]{1,0:T(8,128)(2,1)}, u32[]{:S(2)}) copy-start(bf16[256,64]{1,0:T(8,128)(2,1)} %constant.33.clone.inv_x_ref) | copy-start | bytes 98308
  13.1 20.9 %all-to-all-start = ((bf16[64,2,128]{2,1,0:T(2,128)(2,1)}), bf16[64,2,128]{2,1,0:T(2,128)(2,1)S(1)}, u32[]{:S(2)}, u32[]{:S(2)}) async-start(bf16[64,2,128]{2,1,0:T(2,128)(2,1)} %bitcast.1), calls=%async_computation | async-start | bytes 65536 | tf_op jit(solution)/shard_map/all_to_all | solution.py:318
  52.7 1.2 copy-start.6
  53.9 0.9 copy-start.7
  54.9 0.7 copy-start.18
  55.6 0.7 copy-start.19
  56.3 0.7 copy-start.22
  57.0 0.7 copy-start.24
  60.1 26.8 %all-to-all-start.1 = ((bf16[64,16,128]{2,1,0:T(8,128)(2,1)}), bf16[64,16,128]{2,1,0:T(8,128)(2,1)S(1)}, u32[]{:S(2)}, u32[]{:S(2)}) async-start(bf16[64,16,128]{2,1,0:T(8,128)(2,1)} %bitcast.5), calls=%async_computation.1 | async-start | bytes 524288 | tf_op jit(solution)/shard_map/all_to_all | solution.py:318
  75.9 0.7 copy-start.16
  87.0 1.2 copy-start.9
  88.2 0.9 copy-start.17
  96.7 1.3 copy-start.1
  98.0 0.7 copy-start.13
  98.7 18.0 %all-to-all-start.2 = ((bf16[64,16,128]{2,1,0:T(8,128)(2,1)}), bf16[64,16,128]{2,1,0:T(8,128)(2,1)S(1)}, u32[]{:S(2)}, u32[]{:S(2)}) async-start(bf16[64,16,128]{2,1,0:T(8,128)(2,1)} %bitcast.15), calls=%async_computation.2 | async-start | bytes 524288 | tf_op jit(solution)/shard_map/all_to_all | solution.py:318
  116.8 22.3 %copy-start.2 = (bf16[32,2,128,128]{3,2,1,0:T(8,128)(2,1)S(1)}, bf16[32,2,128,128]{3,2,1,0:T(8,128)(2,1)}, u32[]{:S(2)}) copy-start(bf16[32,2,128,128]{3,2,1,0:T(8,128)(2,1)} %copy-done.1) | copy-start | bytes 6291460
  116.8 1.4 copy-start.3
  118.1 0.9 copy-start.8
  119.1 0.9 copy-start.11
Sparse Core Ops, SparseCore 0:
  9.4 43.1 all-gather.2
  54.8 40.1 all-gather.4
where the time goes:
time: 152 us
  waiting for transfers between devices  49.5 us (33%)
  starting transfers between devices  32.5 us (21%)
  Pallas kernels  19.2 us (13%)
  local copies, waits for them, and re-layouts  18.3 us (12%)
  blocking collectives  17.8 us (12%)
  between operations  13.6 us (9%)
    all_to_all x3, starting transfers between devices, exchange(): lax.all_to_all(value, 'slab', split_axis=0, concat_axis=0, tiled=True)  32.5 us
    all_to_all x3, waiting for transfers between devices, exchange(): lax.all_to_all(value, 'slab', split_axis=0, concat_axis=0, tiled=True)  30.8 us
    all_gather x2, waiting for transfers between devices, on_device(): gathered.append(lax.all_gather(local, 'section', axis=0))  18.7 us
    all_to_all x1, blocking collectives, exchange(): lax.all_to_all(value, 'slab', split_axis=0, concat_axis=0, tiled=True)  17.8 us
    unnamed x52, local copies, waits for them, and re-layouts  15.7 us
    pallas_call x1, Pallas kernels, on_device(): call(middle_kernel, 'middle', 9, [jax.ShapeDtypeStruct((32, 2, 128, 128),...  7.55 us
    pallas_call x1, Pallas kernels, on_device(): call(last_kernel, 'last', 6, [jax.ShapeDtypeStruct((1, 32, 2, 128, 128),...  5.75 us
  transfers between devices with their start and end apart: 5, of which 4 were waited for; matrix products, arithmetic and copies ran while one was open for 1% of the time, Pallas kernels for 8%

commit v1 on v0

v1 whole, which is shorter than its diff:
```python
import math

import jax
import jax.numpy as jnp
import ml_dtypes
import numpy as np
from jax import lax
from jax.experimental import pallas as pl
from jax.experimental.pallas import tpu as pltpu
from jax.sharding import PartitionSpec as P

K = 16
HALF = 2 * K
LENGTH = 128
SLABS = 64
BF = jnp.bfloat16
F32 = jnp.float32


def wave(freqs):
    where = np.arange(LENGTH, dtype=np.int64)[None, :]
    step = (freqs % LENGTH)[:, None] * where % LENGTH
    phase = step.astype(np.float32) * np.float32(2.0 * math.pi / LENGTH)
    cosine = np.cos(phase).astype(ml_dtypes.bfloat16).astype(np.float32)
    sine = np.sin(phase).astype(ml_dtypes.bfloat16).astype(np.float32)
    return cosine, sine


def make_tables():
    base = np.arange(HALF)
    signed = np.where(base < K, base, base - HALF)
    cos, sin = wave(signed)
    cos_z, sin_z = wave(np.arange(K))
    double = np.where(np.arange(K) == 0, 1.0, 2.0)[:, None]
    table = {}
    table["pair_y"] = np.concatenate([cos, -sin], 0)
    table["fwd_x"] = np.concatenate(
        [np.concatenate([cos, sin], 1), np.concatenate([-sin, cos], 1)], 0
    )
    fwd_z = np.stack([np.stack([cos_z, sin_z], 1), np.stack([-sin_z, cos_z], 1)], 0)
    fwd_z = fwd_z.reshape(2, K, 2, SLABS, 2)
    full = np.einsum("gf,akrsz->gaksfrz", np.eye(4), fwd_z)
    full = full.reshape(4 * HALF, 8, LENGTH).transpose(1, 0, 2).reshape(1024, LENGTH)
    first = np.einsum("akrsz->zaksr", fwd_z).reshape(2 * HALF, SLABS * 2)
    cz, sz = cos_z * double * 0.25, sin_z * double * 0.25
    inv_z = np.stack([np.stack([cz, -sz], 0), np.stack([sz, cz], 0)], 0)
    inv_z = inv_z.reshape(2, 2, K, SLABS, 2)
    back = np.einsum("gf,arksz->sgazfrk", np.eye(4), inv_z).reshape(SLABS * 16, 4 * HALF)
    table["z"] = np.concatenate([back, full, first], 0)
    inv_x = np.stack([np.stack([cos, -sin], 0), np.stack([sin, cos], 0)], 0)
    table["inv_x"] = np.einsum("arpx->axrp", inv_x).reshape(2 * LENGTH, 2 * HALF) * 0.125
    table["x"] = np.concatenate([table["fwd_x"], np.pad(table.pop("inv_x"), ((0, 0), (0, 192)))], 0)
    one_x = (cos.sum(1) - 1j * sin.sum(1)) / math.sqrt(LENGTH)
    one_z = (cos_z.sum(1) - 1j * sin_z.sum(1)) / math.sqrt(LENGTH)
    return table, one_x, one_z


def split(value):
    return np.stack([value.real, value.imag], 0).astype(np.float32)


def dot(left, right):
    return jnp.dot(left, right, preferred_element_type=F32)


def nt_dot(left, right):
    return lax.dot_general(left, right, (((1,), (1,)), ((), ())), preferred_element_type=F32)


def picks(rows, cols):
    row = lax.broadcasted_iota(jnp.int32, (rows, cols), 0)
    col = lax.broadcasted_iota(jnp.int32, (rows, cols), 1)
    return row, col


def one_hot(mask):
    return jnp.where(mask, 1.0, 0.0).astype(BF)


def fetch(copies):
    started = [pltpu.make_async_copy(source, target, sem) for source, target, sem in copies]
    for copy in started:
        copy.start()
    return started


def spread_kernel(
    place_ref, one_x_ref, bypass_ref, lift_ref, bypass_bias_ref, lift_bias_ref, pair_y_ref,
    one_y_ref, one_z_ref, z_ref, x_ref, kb_ref, kl_ref, bias_ref, fwd_y_ref, inv_y_ref, ones_ref,
    z_out, x_out,
):
    z_out[...] = z_ref[...]
    x_out[...] = x_ref[...]
    row, col = picks(512, 32)
    expand = one_hot(row // 16 == col)
    row, col = picks(512, 512)
    same = (row % 16) == (col % 16)
    for layer in range(2):
        tall = nt_dot(expand, bypass_ref[layer]).astype(BF)
        kb_ref[layer] = jnp.where(same, nt_dot(tall, expand), 0.0).astype(BF)
    row, col = picks(64, 4)
    expand4 = one_hot(row // 16 == col)
    tall = nt_dot(expand, lift_ref[...]).astype(BF)
    row, col = picks(512, 64)
    kl_ref[:, :64] = jnp.where((row % 16) == (col % 16), nt_dot(tall, expand4), 0.0).astype(BF)
    kl_ref[:, 64:] = jnp.zeros((512, 64), BF)
    filled = jnp.ones((32, LENGTH), BF)
    expand = expand.astype(F32)
    for index in range(3):
        vector = bypass_bias_ref[index : index + 1] if index < 2 else lift_bias_ref[...]
        bias_ref[index] = dot((expand * vector.astype(F32)).astype(BF), filled)
    row, col = picks(512, 64)
    repeat = one_hot((row // 128 == col // 16) & (row % 16 == col % 16))
    tall = dot(repeat, pair_y_ref[...])
    back = (tall * 0.125).astype(BF)
    row, col = picks(512, LENGTH)
    for c in range(8):
        inv_y_ref[:, c * 128 : c * 128 + 128] = jnp.where((row // 16) % 8 == c, back, 0.0).astype(BF)
    wide = tall.T
    row, col = picks(LENGTH, 512)
    for c in range(8):
        block = jnp.where((col // 16) % 8 == c, wide, 0.0).astype(BF)
        fwd_y_ref[c * 128 : c * 128 + 128, :] = block
    place = place_ref[0]
    xr, xi = one_x_ref[place // 2, 0:1, :], one_x_ref[place // 2, 1:2, :]
    yr = jnp.where(place % 2 == 0, one_y_ref[0, 0:1, :], one_y_ref[1, 0:1, :])
    yi = jnp.where(place % 2 == 0, one_y_ref[0, 1:2, :], one_y_ref[1, 1:2, :])
    pr, pi = xr * yr - xi * yi, xr * yi + xi * yr
    zr, zi = one_z_ref[0], one_z_ref[1]
    ones_ref[...] = jnp.concatenate([zr * pr - zi * pi, zr * pi + zi * pr], axis=0)


def fold_kernel(lift_ref, lift_bias_ref, weight_hbm, out_ref, weight, sem):
    (copy,) = fetch([(weight_hbm.at[0], weight, sem.at[0])])
    row, col = picks(HALF, 4)
    pick = one_hot((row % 8 == col))
    row, col = picks(HALF, HALF)
    lift = dot(pick, lift_ref[...]) + jnp.where(row % 8 == 4, lift_bias_ref[...].astype(F32), 0.0)
    row, col = picks(HALF, LENGTH)
    lift = dot(lift.astype(BF), one_hot(row == col // 4))
    lift = jnp.where(row // 8 == col % 4, lift, 0.0).astype(BF)
    copy.wait()
    for r in range(2):
        folded = dot(lift, weight[r]).astype(BF)
        for section in range(8):
            out_ref[section, r * HALF : r * HALF + HALF, :] = folded


def start_kernel(fields_hbm, pair_y_hbm, fwd_x_hbm, out_ref, fields, pair_y, fwd_x, rows, sem):
    copies = fetch(
        [
            (pair_y_hbm, pair_y, sem.at[0]),
            (fields_hbm.at[0], fields, sem.at[1]),
            (fwd_x_hbm, fwd_x, sem.at[2]),
        ]
    )
    copies[0].wait()
    row, col = picks(256, 64)
    repeat = one_hot((row // 64 == col // 16) & (row % 16 == col % 16))
    wide = dot(repeat, pair_y[...]).T
    row, col = picks(LENGTH, 256)
    fwd_y = jnp.concatenate(
        [jnp.where((col // 16) % 4 == c, wide, 0.0).astype(BF) for c in range(4)], axis=0
    )
    lane = lax.broadcasted_iota(jnp.int32, (64, LENGTH), 1)
    copies[1].wait()
    copies[2].wait()
    made = []
    for z in range(2):
        wide = jnp.concatenate([fields[c, z] for c in range(4)], axis=1)
        along = dot(wide, fwd_y).astype(BF)
        stacked = jnp.concatenate([along[:, :128], along[:, 128:]], axis=0)
        made.append(dot(fwd_x[...], stacked) * (1.0 / LENGTH))
    first = jnp.where(lane < 64, made[0], pltpu.roll(made[1], 64, 1))
    second = jnp.where(lane < 64, pltpu.roll(made[0], 64, 1), made[1])
    for h, value in enumerate((first, second)):
        for r in range(2):
            rows[pl.ds(h * 2 + r, 32, stride=4), :] = value[r * 32 : r * 32 + 32]
    out_ref[...] = rows[...].astype(BF)


def mix(weight_ref, modes, pattern):
    low = lax.broadcasted_iota(jnp.int32, (8, LENGTH), 0) < 4
    for pair in range(16):
        for r in range(2):
            for half in range(2):
                even = jnp.broadcast_to(modes[r, half, 2 * pair : 2 * pair + 1, :], (8, LENGTH))
                odd = jnp.broadcast_to(modes[r, half, 2 * pair + 1 : 2 * pair + 2, :], (8, LENGTH))
                pattern[pair, r, half] = jnp.where(low, even, odd)
    mixed = {}
    for g in range(4):
        total = {}
        for side in range(2):
            section = 2 * g + side
            acc = [[jnp.zeros((8, LENGTH), F32) for _ in range(2)] for _ in range(2)]
            for quad in range(8):
                real = weight_ref[section, 0, quad * 16 : quad * 16 + 16, :].astype(F32)
                imag = weight_ref[section, 1, quad * 16 : quad * 16 + 16, :].astype(F32)
                for sub in range(2):
                    pair = quad * 2 + sub
                    for half in range(2):
                        wr = real[sub * 8 : sub * 8 + 8, half * 128 : half * 128 + 128]
                        wi = imag[sub * 8 : sub * 8 + 8, half * 128 : half * 128 + 128]
                        mr, mi = pattern[pair, 0, half], pattern[pair, 1, half]
                        acc[0][half] = acc[0][half] + wr * mr - wi * mi
                        acc[1][half] = acc[1][half] + wr * mi + wi * mr
            for r in range(2):
                for half in range(2):
                    value = acc[r][half]
                    total[side, r, half] = value + pltpu.roll(value, 4, 0)
        for r in range(2):
            for half in range(2):
                mixed[g, r, half] = jnp.where(low, total[0, r, half], total[1, r, half])
    return mixed


def first_mix(folded_ref, modes):
    sub = lax.broadcasted_iota(jnp.int32, (8, LENGTH), 0)
    mixed = {}
    for g in range(4):
        for row in range(0, 8, 2):
            section, o = 2 * g + row // 4, row % 4
            real = folded_ref[section, o * 8 : o * 8 + 16, :].astype(F32)
            imag = folded_ref[section, HALF + o * 8 : HALF + o * 8 + 16, :].astype(F32)
            for more in range(2):
                for half in range(2):
                    wr = real[more * 8 : more * 8 + 8, half * 128 : half * 128 + 128]
                    wi = imag[more * 8 : more * 8 + 8, half * 128 : half * 128 + 128]
                    mr, mi = modes[0, half], modes[1, half]
                    for r, value in enumerate((wr * mr - wi * mi, wr * mi + wi * mr)):
                        for step in (4, 2, 1):
                            value = value + pltpu.roll(value, step, 0)
                        if row + more:
                            value = jnp.where(sub == row + more, value, mixed[g, r, half])
                        mixed[g, r, half] = value
    return mixed


def evaluate(mixed, turned, z_ref, out_ref):
    slot = lax.broadcasted_iota(jnp.int32, (8, LENGTH), 1) // K
    for py in range(K):
        half, at = py // 8, py % 8
        value = None
        for g in range(4):
            for r in range(2):
                where = 2 * g + r
                moved = mixed[g, r, half]
                if where != at:
                    moved = pltpu.roll(moved, (where - at) * K % LENGTH, 1)
                value = moved if value is None else jnp.where(slot == where, moved, value)
        turned[pl.ds(py, 8, stride=K), :] = value
    out_ref[...] = nt_dot(z_ref[:1024], turned[...].astype(BF)).astype(BF)


def unravel(turned, groups, modes):
    slot = lax.broadcasted_iota(jnp.int32, (8, LENGTH), 1) // K
    parts = [turned[pl.ds(py, 8, stride=K), :] for py in range(K)]
    for g in range(groups):
        for r in range(2):
            source = 2 * g + r
            for half in range(2):
                value = None
                for at in range(8):
                    moved = parts[half * 8 + at]
                    if at != source:
                        moved = pltpu.roll(moved, (at - source) * K % LENGTH, 1)
                    value = moved if value is None else jnp.where(slot == at, moved, value)
                modes[r, half, g * 8 : g * 8 + 8, :] = value


def dropped(place_ref, shape):
    row = lax.broadcasted_iota(jnp.int32, shape, 0)
    lane = lax.broadcasted_iota(jnp.int32, shape, 1)
    origin = jnp.logical_and(row % K == 0, lane % K == 0)
    return jnp.logical_and(origin, place_ref[0] == 0)


def first_mix_kernel(
    place_ref, got_ref, folded_ref, ones_ref, z_ref, out_ref, turned, modes
):
    both = dot(z_ref[2048:], got_ref[...])
    lane = lax.broadcasted_iota(jnp.int32, (HALF, LENGTH), 1)
    value = both[:HALF] + pltpu.roll(both[HALF:], 64, 1)
    value = jnp.where(lane < 64, value, 0.0) * (1.0 / math.sqrt(LENGTH))
    value = jnp.where(lane // K == 4, ones_ref[...], value)
    value = jnp.where(dropped(place_ref, value.shape), 0.0, value)
    value = jnp.concatenate([value, jnp.zeros((LENGTH - HALF, LENGTH), F32)], axis=0)
    turned[...] = value.T
    unravel(turned, 1, modes)
    evaluate(first_mix(folded_ref, modes), turned, z_ref, out_ref)


def mix_kernel(
    place_ref, got_ref, z_ref, weight_hbm, out_ref, weight, turned, modes, pattern, sem
):
    (copy,) = fetch([(weight_hbm, weight, sem.at[0])])
    value = None
    for block in range(8):
        span = slice(block * 128, block * 128 + 128)
        part = dot(z_ref[1024 + block * 128 : 1152 + block * 128], got_ref[span])
        value = part if value is None else value + part
    value = value * (1.0 / math.sqrt(LENGTH))
    value = jnp.where(dropped(place_ref, value.shape), 0.0, value)
    turned[...] = value.T
    unravel(turned, 4, modes)
    copy.wait()
    evaluate(mix(weight, modes, pattern), turned, z_ref, out_ref)


def inverse(got_ref, x_ref, inv_y_ref, rows, field):
    rows[...] = got_ref[...].astype(F32)
    for g in range(4):
        for z in range(2):
            parts = []
            for h in range(2):
                pieces = [
                    rows[pl.ds(h * 16 + g * 4 + r * 2 + z, 32, stride=32), :] for r in range(2)
                ]
                parts.append(jnp.concatenate(pieces, axis=0).astype(BF))
            along = dot(x_ref[64:, :64], jnp.concatenate(parts, axis=1)).astype(BF)
            wide = jnp.concatenate([along[:128], along[128:]], axis=1)
            made = dot(wide, inv_y_ref[...])
            for o in range(8):
                field[g * 8 + o, z] = made[:, o * 128 : o * 128 + 128]


def activate(value):
    inner = value * (0.7978845608028654 + 0.035677408136300125 * value * value)
    half = 0.5 * value
    return half + half * jnp.tanh(inner)


def pointwise(block, hidden, kb_ref, bias, field):
    bypassed = dot(kb_ref[...], hidden)
    made = []
    for z in range(2):
        part = field[:, z, block * 16 : block * 16 + 16, :].reshape(512, LENGTH)
        value = bypassed[:, z * 128 : z * 128 + 128] + bias + part
        made.append(activate(value).astype(BF))
    return made


def middle_kernel(
    got_ref, kl_ref, kb_ref, bias_ref, inv_y_ref, fwd_y_ref, x_ref, fields_hbm, hidden_hbm, out_ref,
    fields, rows, field, hidden, sem,
):
    (copy,) = fetch([(fields_hbm.at[0], fields, sem.at[0])])
    inverse(got_ref, x_ref, inv_y_ref, rows, field)
    lift_bias = bias_ref[2]
    lift_bias = jnp.concatenate([lift_bias, lift_bias], axis=1)
    copy.wait()
    for block in range(8):
        span = slice(block * 16, block * 16 + 16)
        raw = [fields[:, z, span, :].reshape(64, LENGTH) for z in range(2)]
        lifted = dot(kl_ref[:, :64], jnp.concatenate(raw, axis=1)) + lift_bias
        made = pointwise(block, lifted.astype(BF), kb_ref.at[0], bias_ref[0], field)
        for z in range(2):
            hidden[:, z, span, :] = made[z].reshape(32, 16, LENGTH)
    (kept,) = fetch([(hidden, hidden_hbm, sem.at[1])])
    for g in range(4):
        for z in range(2):
            wide = jnp.concatenate([hidden[g * 8 + c, z] for c in range(8)], axis=1)
            along = dot(wide, fwd_y_ref[...]).astype(BF)
            stacked = jnp.concatenate([along[:, :256], along[:, 256:]], axis=0)
            spectrum = dot(x_ref[:64], stacked) * (1.0 / LENGTH)
            for h in range(2):
                for r in range(2):
                    at = h * 16 + g * 4 + r * 2 + z
                    rows[pl.ds(at, 32, stride=32), :] = spectrum[
                        r * 32 : r * 32 + 32, h * 128 : h * 128 + 128
                    ]
    out_ref[...] = rows[...].astype(BF)
    kept.wait()


def last_kernel(
    got_ref, kb_ref, bias_ref, inv_y_ref, x_ref, hidden_hbm, out_hbm, hidden, rows, field, made_ref,
    sem,
):
    (copy,) = fetch([(hidden_hbm, hidden, sem.at[0])])
    inverse(got_ref, x_ref, inv_y_ref, rows, field)
    copy.wait()
    kept = []
    for block in range(8):
        span = slice(block * 16, block * 16 + 16)
        raw = [hidden[:, z, span, :].reshape(512, LENGTH) for z in range(2)]
        made = pointwise(block, jnp.concatenate(raw, axis=1), kb_ref.at[1], bias_ref[1], field)
        for z in range(2):
            made_ref[:, z, span, :] = made[z].reshape(32, 16, LENGTH)
        kept += fetch([(made_ref.at[:, :, span, :], out_hbm.at[0, :, :, span, :], sem.at[1 + block])])
    for copy in kept:
        copy.wait()


def call(kernel, name, inputs, outputs, scratch, sems=0, limit=24):
    spaces = {"s": pltpu.SMEM, "v": pltpu.VMEM, "p": pltpu.VMEM, "h": pltpu.HBM, "f": pltpu.HBM}
    fetched = [index for index, letter in enumerate(inputs) if letter == "f"]

    def run(*arrays):
        buffers = [pltpu.VMEM(arrays[index].shape, arrays[index].dtype) for index in fetched]
        own = [pltpu.VMEM(shape, kind) for shape, kind in scratch]
        if sems:
            own.append(pltpu.SemaphoreType.DMA((sems,)))
        if fetched:
            buffers.append(pltpu.SemaphoreType.DMA((len(fetched),)))

        def body(*refs):
            refs = list(refs)
            if fetched:
                first = len(inputs) + len(outputs) + len(own)
                copies = []
                for order, index in enumerate(fetched):
                    copies.append((refs[index], refs[first + order], refs[-1].at[order]))
                    refs[index] = refs[first + order]
                for copy in fetch(copies):
                    copy.wait()
                refs = refs[:first]
            kernel(*refs)

        placed = []
        for letter, array in zip(inputs, arrays):
            if letter in "hfp":
                array = pltpu.with_memory_space_constraint(array, spaces[letter])
            placed.append(array)
        return pl.pallas_call(
            body,
            name=name,
            out_shape=[spaces[letter](shape, kind) for letter, shape, kind in outputs],
            in_specs=[pl.BlockSpec(memory_space=spaces[letter]) for letter in inputs],
            out_specs=[pl.BlockSpec(memory_space=spaces[letter]) for letter, _, _ in outputs],
            scratch_shapes=own + buffers,
            compiler_params=pltpu.CompilerParams(vmem_limit_bytes=limit << 20),
        )(*placed)

    return run


def exchange(value, axis="slab"):
    return lax.all_to_all(value, axis, split_axis=0, concat_axis=0, tiled=True)


tie = lax.optimization_barrier


def solution(mesh):
    table, one_x, one_z = make_tables()
    const = {name: value.astype(ml_dtypes.bfloat16) for name, value in table.items()}
    ones_x = np.repeat(split(one_x).T[:, :, None], LENGTH, axis=2)
    ones_y = np.tile(split(one_x).reshape(2, 2, 1, K), (1, 1, 8, 1)).reshape(2, 2, LENGTH)
    ones_y = ones_y.transpose(1, 0, 2)
    ones_z = np.repeat(split(one_z)[:, :, None], LENGTH, axis=2)

    def on_device(fields, lift_weight, lift_bias, spectral_weight, bypass_weight, bypass_bias):
        place = lax.axis_index("slab").reshape(1)
        lift_bias = lift_bias[None]
        packed, cube = (1024, LENGTH), (32, 2, 128, 128)
        (spectrum,) = call(
            start_kernel,
            "start",
            "hhh",
            [("v", (128, LENGTH), BF)],
            [((4, 2, 128, 128), BF), ((64, 128), BF), ((64, 256), BF), ((128, 128), F32)],
            sems=3,
        )(fields, const["pair_y"], const["fwd_x"])
        spectrum, spectral_weight, bypass_weight = tie((spectrum, spectral_weight, bypass_weight))
        spectrum = exchange(spectrum)
        weight = spectral_weight.reshape(2, 2, LENGTH, 256)
        (folded,) = call(
            fold_kernel, "fold", "ffh", [("v", (8, 64, 256), BF)], [((2, 128, 256), BF)], sems=1
        )(lift_weight, lift_bias, weight)
        kb, kl, bias, fwd_y, inv_y, ones, z_table, x_table = call(
            spread_kernel,
            "spread",
            "s" + "f" * 10,
            [
                ("v", (2, 512, 512), BF),
                ("v", (512, 128), BF),
                ("v", (3, 512, LENGTH), F32),
                ("v", (1024, 512), BF),
                ("v", (512, 1024), BF),
                ("v", (HALF, LENGTH), F32),
                ("v", (2112, 128), BF),
                ("v", (320, 256), BF),
            ],
            [],
        )(
            place, ones_x, bypass_weight, lift_weight, bypass_bias, lift_bias, const["pair_y"],
            ones_y, ones_z, const["z"], const["x"],
        )
        later = weight[1]
        folded, ones, later, _ = tie((folded, ones, later, spectrum))
        folded = exchange(folded.reshape(512, 256), "section").reshape(8, 64, 256)
        _, later = tie((folded, later))
        gathered = lax.all_gather(later, "section", axis=0)
        (planes,) = call(
            first_mix_kernel,
            "mix0",
            "spppp",
            [("v", packed, BF)],
            [((128, 128), F32), ((2, 2, 8, 128), F32)],
        )(place, spectrum, folded, ones, z_table)
        hidden, spectrum = call(
            middle_kernel,
            "middle",
            "ppppppph",
            [("h", cube, BF), ("v", packed, BF)],
            [((4, 2, 128, 128), BF), (packed, F32), (cube, F32), (cube, BF)],
            sems=2,
        )(exchange(planes), kl, kb, bias, inv_y, fwd_y, x_table, fields)
        (planes,) = call(
            mix_kernel,
            "mix1",
            "spph",
            [("v", packed, BF)],
            [
                ((8, 2, 128, 256), BF), ((128, 128), F32), ((2, 2, 32, 128), F32),
                ((16, 2, 2, 8, 128), F32),
            ],
            sems=1,
        )(place, exchange(spectrum), z_table, gathered)
        (features,) = call(
            last_kernel,
            "last",
            "ppppph",
            [("h", (1,) + cube, BF)],
            [(cube, BF), (packed, F32), (cube, F32), (cube, BF)],
            sems=9,
        )(exchange(planes), kb, bias, inv_y, x_table, hidden)
        return features

    placed = (
        P("section", None, "slab", None, None),
        P(),
        P(),
        P(None, None, None, "section", "slab"),
        P(),
        P(),
    )
    return jax.shard_map(
        on_device,
        mesh=mesh,
        in_specs=placed,
        out_specs=P("section", None, "slab", None, None),
        check_vma=False,
    )
```

time: 152 us -> 142 us (0.934)
  blocking collectives: 17.8 us -> 80.5 us
  waiting for transfers between devices: 49.5 us -> 0.02 us
  starting transfers between devices: 32.5 us -> 11.9 us
  local copies, waits for them, and re-layouts: 18.3 us -> 9.81 us
  Pallas kernels: 19.2 us -> 26 us
    all_to_all x1 -> x4, blocking collectives: 17.8 us -> 80.5 us  [exchange(): return lax.all_to_all(value, axis, split_axis=0, concat_axis=0, tiled=True)]
    all_to_all x3 -> x1, waiting for transfers between devices: 30.8 us -> 0.01 us  [exchange(): return lax.all_to_all(value, axis, split_axis=0, concat_axis=0, tiled=True)]
    all_to_all x3 -> x1, starting transfers between devices: 32.5 us -> 11.8 us  [exchange(): return lax.all_to_all(value, axis, split_axis=0, concat_axis=0, tiled=True)]
    all_gather x2 -> x1, waiting for transfers between devices: 18.7 us -> 0.01 us  [on_device(): gathered = lax.all_gather(later, 'section', axis=0)]
    unnamed x52 -> x20, local copies, waits for them, and re-layouts: 15.7 us -> 6.45 us
    pallas_call x6 -> x7, Pallas kernels: 19.2 us -> 26 us  [run(): pl.pallas_call(body, name=name, out_shape=[spaces[letter](shape, kind) fo...]
    reshape x0 -> x1, local copies, waits for them, and re-layouts: none -> 1.72 us  [on_device(): weight = spectral_weight.reshape(2, 2, LENGTH, 256)]
  transfers between devices with their start and end apart: 5 -> 2, of which waited for: 4 -> 0; matrix products, arithmetic and copies ran while one was open for 1% -> 2% of each run, Pallas kernels for 8% -> 10%
where the time goes in v1:
time: 142 us
  blocking collectives  80.5 us (57%)
  Pallas kernels  26 us (18%)
  between operations  13.5 us (10%)
  starting transfers between devices  11.9 us (8%)
  local copies, waits for them, and re-layouts  9.81 us (7%)
    all_to_all x4, blocking collectives, exchange(): return lax.all_to_all(value, axis, split_axis=0, concat_axis=0, tiled=True)  80.5 us
    pallas_call x7, Pallas kernels, run(): pl.pallas_call(body, name=name, out_shape=[spaces[letter](shape, kind) fo...  26 us
    all_to_all x1, starting transfers between devices, exchange(): return lax.all_to_all(value, axis, split_axis=0, concat_axis=0, tiled=True)  11.8 us
    unnamed x20, local copies, waits for them, and re-layouts  6.45 us
  transfers between devices with their start and end apart: 2, of which 0 were waited for; matrix products, arithmetic and copies ran while one was open for 2% of the time, Pallas kernels for 10%

profile of v1, /device:TPU:1, one launch (start us, length us, event | category | flops | bytes accessed | tf_op | source)
XLA Modules:
  0.0 141.7 jit_solution(16516561557407877566)
XLA Ops:
  6.5 2.2 %start.1 = bf16[128,128]{1,0:T(8,128)(2,1)} custom-call(bf16[1,4,2,128,128]{4,3,2,1,0:T(8,128)(2,1)} %refs_7_.2, bf16[64,128]{1,0:T(8,128)(2,1)} %constant.18.clone.refs_1_.refs_6_, bf16[64,256]{1,0:T(8,128)(2,1)} %constant.19.clone.refs_2_), custom_call_target="tpu_custom_call" | custom-call | tf_op jit(solution)/shard_map/start/pallas_call | solution.py:425
  8.8 11.8 %all-to-all-start = ((bf16[64,2,128]{2,1,0:T(2,128)(2,1)}), bf16[64,2,128]{2,1,0:T(2,128)(2,1)}, u32[]{:S(2)}, u32[]{:S(2)}) async-start(bf16[64,2,128]{2,1,0:T(2,128)(2,1)} %bitcast.1), calls=%async_computation | async-start | bytes 65536 | tf_op jit(solution)/shard_map/all_to_all | solution.py:439
  20.6 0.0 all-gather.3.cloned.1.call-start
  20.7 1.7 %reshape.23.refs_2_ = bf16[2,2,128,256]{3,2,1,0:T(8,128)(2,1)} reshape(bf16[2,2,32,4,256]{4,3,2,1,0:T(4,128)(2,1)} %param.16) | data formatting | bytes 524288 | tf_op jit(solution)/shard_map/reshape | solution.py:467
  22.4 0.9 slice.4
  23.4 0.7 squeeze.3
  24.0 1.8 %fold.1 = bf16[8,64,256]{2,1,0:T(8,128)(2,1)S(1)} custom-call(bf16[4,32]{1,0:T(4,128)(2,1)} %refs_3_.1, bf16[1,32]{1,0:T(2,128)(2,1)} %bitcast.18, bf16[2,2,128,256]{3,2,1,0:T(8,128)(2,1)} %reshape.23.refs_2_), custom_call_target="tpu_custom_call" | custom-call | tf_op jit(solution)/shard_map/fold/pallas_call | solution.py:425
  25.8 0.0 copy-start.1
  25.8 0.7 copy-done.1
  26.5 2.6 %spread.1 = (bf16[2,512,512]{2,1,0:T(8,128)(2,1)S(1)}, bf16[512,128]{1,0:T(8,128)(2,1)S(1)}, f32[3,512,128]{2,1,0:T(8,128)S(1)}, bf16[1024,512]{1,0:T(8,128)(2,1...) custom-call(s32[1]{0:T(128)} %bitcast.refs_0_, ...), custom_call_target="tpu_custom_call" | custom-call | tf_op jit(solution)/shard_map/spread/pallas_call | solution.py:425
  29.1 0.0 copy-start.3
  29.1 1.0 copy-done.3
  30.1 0.0 copy-start.5
  30.1 0.7 copy-done.5
  30.8 0.0 copy-start.8
  30.8 0.6 copy-done.8
  31.4 0.0 all-to-all-done
  31.4 20.8 %all_to_all.50.refs_2_ = bf16[8,64,256]{2,1,0:T(8,128)(2,1)} all-to-all(bf16[8,64,256]{2,1,0:T(8,128)(2,1)} %copy-done.1), channel_id=1, replica_groups=mesh['section'=8,'slab'=64] {'section'}, dimensions={0} | all-to-all | bytes 524288 | tf_op jit(solution)/shard_map/all_to_all | solution.py:439
  52.1 0.0 all-gather.3.cloned.1.call-update
  52.2 0.0 copy-start.2
  52.2 0.9 copy-done.2
  53.1 0.0 copy-start.9
  53.1 0.7 copy-done.9
  53.8 0.0 copy-start.4
  53.8 1.8 %mix0.1 = bf16[1024,128]{1,0:T(8,128)(2,1)S(1)} custom-call(s32[1]{0:T(128)} %bitcast.refs_0_, bf16[128,128]{1,0:T(8,128)(2,1)} %bitcast.2.refs_1_, bf16[8,64,256]{2,1,0:T(8,128)(2,1)S(1)} %copy-done.2, f32[32,128]{1,0:T(8,128)S(1)} %copy-done.9, bf16[2112,128]{1,0:T(8,128)(2,1)S(1)} %get-tuple-element.28.refs_4_.refs_2_), custom_call_target="tpu_custom_call" | custom-call | tf_op jit(solution)/shard_map/mix0/pallas_call | solution.py:425
  55.6 23.9 %all_to_all.51 = bf16[64,16,128]{2,1,0:T(8,128)(2,1)S(1)} all-to-all(bf16[64,16,128]{2,1,0:T(8,128)(2,1)S(1)} %bitcast.15), channel_id=1, replica_groups=mesh['section'=8,'slab'=64] {'slab'}, dimensions={0} | all-to-all | bytes 524288 | tf_op jit(solution)/shard_map/all_to_all | solution.py:439
  79.6 0.0 copy-done.4
  79.6 0.0 copy-start.6
  79.6 0.9 copy-done.6
  80.5 8.6 %middle.1 = (bf16[32,2,128,128]{3,2,1,0:T(8,128)(2,1)}, bf16[1024,128]{1,0:T(8,128)(2,1)S(1)}) custom-call(bf16[1024,128]{1,0:T(8,128)(2,1)S(1)} %bitcast.13, bf16[512,128]{1,0:T(8,128)(2,1)S(1)} %get-tuple-element.29.refs_1_, bf16[2,512,512]{2,1,0:T(8,128)(2,1)S(1)} %get-tuple-element.30.refs_2_.refs_1_, ...), custom_call_target="tpu_custom_call" | custom-call | tf_op jit(solution)/shard_map/middle/pallas_call | solution.py:425
  89.1 17.9 %all_to_all.52 = bf16[64,16,128]{2,1,0:T(8,128)(2,1)} all-to-all(bf16[64,16,128]{2,1,0:T(8,128)(2,1)S(1)} %bitcast.16), channel_id=1, replica_groups=mesh['section'=8,'slab'=64] {'slab'}, dimensions={0} | all-to-all | bytes 524288 | tf_op jit(solution)/shard_map/all_to_all | solution.py:439
  107.0 0.0 all-gather.3.cloned.1.call-done
  107.0 0.0 copy-start
  107.0 0.9 copy-done
  108.0 0.0 copy-start.7
  108.0 2.0 %mix1.1 = bf16[1024,128]{1,0:T(8,128)(2,1)S(1)} custom-call(s32[1]{0:T(128)} %bitcast.refs_0_, bf16[1024,128]{1,0:T(8,128)(2,1)S(1)} %bitcast.11, bf16[2112,128]{1,0:T(8,128)(2,1)S(1)} %get-tuple-element.28.refs_4_.refs_2_, bf16[8,2,128,256]{3,2,1,0:T(8,128)(2,1)} %bitcast.17), custom_call_target="tpu_custom_call" | custom-call | tf_op jit(solution)/shard_map/mix1/pallas_call | solution.py:425
  110.0 17.8 %all_to_all.53 = bf16[64,16,128]{2,1,0:T(8,128)(2,1)S(1)} all-to-all(bf16[64,16,128]{2,1,0:T(8,128)(2,1)S(1)} %bitcast.14), channel_id=1, replica_groups=mesh['section'=8,'slab'=64] {'slab'}, dimensions={0} | all-to-all | bytes 524288 | tf_op jit(solution)/shard_map/all_to_all | solution.py:439
  127.9 0.0 copy-done.7
  127.9 7.0 %last.1 = bf16[1,32,2,128,128]{4,3,2,1,0:T(8,128)(2,1)} custom-call(bf16[1024,128]{1,0:T(8,128)(2,1)S(1)} %bitcast.12, bf16[2,512,512]{2,1,0:T(8,128)(2,1)S(1)} %get-tuple-element.30.refs_2_.refs_1_, f32[3,512,128]{2,1,0:T(8,128)S(1)} %get-tuple-element.31.refs_3_.refs_2_, bf16[512,1024]{1,0:T(8,128)(2,1)S(1)} %get-tuple-element.32.refs_4_.refs_3_, ...), custom_call_target="tpu_custom_call" | custom-call | tf_op jit(solution)/shard_map/last/pallas_call | solution.py:425
Async XLA Ops:
  8.8 22.6 %all-to-all-start = ((bf16[64,2,128]{2,1,0:T(2,128)(2,1)}), bf16[64,2,128]{2,1,0:T(2,128)(2,1)}, u32[]{:S(2)}, u32[]{:S(2)}) async-start(bf16[64,2,128]{2,1,0:T(2,128)(2,1)} %bitcast.1), calls=%async_computation | async-start | bytes 65536 | tf_op jit(solution)/shard_map/all_to_all | solution.py:439
  20.6 86.4 %all-gather.3.cloned.1.call-start = ((), (), s32[]{:S(2)}) async-start(), calls=%async_computation.5 | async-start | bytes 1179648 | tf_op jit(solution)/shard_map/all_gather | solution.py:494
  25.8 0.7 copy-start.1
  29.1 1.0 copy-start.3
  30.1 0.7 copy-start.5
  30.8 0.6 copy-start.8
  52.2 1.0 copy-start.2
  53.1 0.7 copy-start.9
  53.8 25.7 %copy-start.4 = (bf16[1024,512]{1,0:T(8,128)(2,1)S(1)}, bf16[1024,512]{1,0:T(8,128)(2,1)}, u32[]{:S(2)}) copy-start(bf16[1024,512]{1,0:T(8,128)(2,1)} %copy-done.3) | copy-start | bytes 3145732
  79.6 0.9 copy-start.6
  107.0 1.0 copy-start
  108.0 19.9 %copy-start.7 = (bf16[320,256]{1,0:T(8,128)(2,1)S(1)}, bf16[320,256]{1,0:T(8,128)(2,1)}, u32[]{:S(2)}) copy-start(bf16[320,256]{1,0:T(8,128)(2,1)} %copy-done.5) | copy-start | bytes 491524
Sparse Core Ops, SparseCore 0:
  52.3 35.2 all-gather.2

commit v2 on v1

--- a/solution.py
+++ b/solution.py
@@ -86,7 +86,7 @@
 
 def spread_kernel(
     place_ref, one_x_ref, bypass_ref, lift_ref, bypass_bias_ref, lift_bias_ref, pair_y_ref,
-    one_y_ref, one_z_ref, z_ref, x_ref, kb_ref, kl_ref, bias_ref, fwd_y_ref, inv_y_ref, ones_ref,
+    one_y_ref, one_z_ref, z_ref, x_ref, kb_ref, kc_ref, bias_ref, fwd_y_ref, inv_y_ref, ones_ref,
     z_out, x_out,
 ):
     z_out[...] = z_ref[...]
@@ -94,32 +94,45 @@
     row, col = picks(512, 32)
     expand = one_hot(row // 16 == col)
     row, col = picks(512, 512)
-    same = (row % 16) == (col % 16)
-    for layer in range(2):
-        tall = nt_dot(expand, bypass_ref[layer]).astype(BF)
-        kb_ref[layer] = jnp.where(same, nt_dot(tall, expand), 0.0).astype(BF)
+    tall = nt_dot(expand, bypass_ref[1]).astype(BF)
+    kb_ref[...] = jnp.where((row % 16) == (col % 16), nt_dot(tall, expand), 0.0).astype(BF)
+    joint = dot(lift_ref[...], bypass_ref[0])
+    high = joint.astype(BF)
+    low = (joint - high.astype(F32)).astype(BF)
     row, col = picks(64, 4)
     expand4 = one_hot(row // 16 == col)
-    tall = nt_dot(expand, lift_ref[...]).astype(BF)
     row, col = picks(512, 64)
-    kl_ref[:, :64] = jnp.where((row % 16) == (col % 16), nt_dot(tall, expand4), 0.0).astype(BF)
-    kl_ref[:, 64:] = jnp.zeros((512, 64), BF)
+    for index, part in enumerate((high, low)):
+        wide = nt_dot(nt_dot(expand, part).astype(BF), expand4)
+        wide = jnp.where((row % 16) == (col % 16), wide, 0.0).astype(BF)
+        kc_ref[:, index * 64 : index * 64 + 64] = wide
     filled = jnp.ones((32, LENGTH), BF)
-    expand = expand.astype(F32)
-    for index in range(3):
-        vector = bypass_bias_ref[index : index + 1] if index < 2 else lift_bias_ref[...]
-        bias_ref[index] = dot((expand * vector.astype(F32)).astype(BF), filled)
-    row, col = picks(512, 64)
-    repeat = one_hot((row // 128 == col // 16) & (row % 16 == col % 16))
+    row, col = picks(32, 32)
+    eye = jnp.where(row == col, 1.0, 0.0)
+
+    def column(vector):
+        return dot((eye * vector.astype(F32)).astype(BF), filled)
+
+    shift = column(bypass_bias_ref[0:1]) + lax.dot_general(
+        bypass_ref[0], column(lift_bias_ref[...]).astype(BF), (((0,), (0,)), ((), ())),
+        preferred_element_type=F32,
+    )
+    for index, value in enumerate((shift, column(bypass_bias_ref[1:2]))):
+        bias_ref[index] = jnp.dot(
+            expand.astype(F32), value, precision=lax.Precision.HIGHEST, preferred_element_type=F32
+        )
+    row, col = picks(256, 64)
+    repeat = one_hot((row // 64 == col // 16) & (row % 16 == col % 16))
     tall = dot(repeat, pair_y_ref[...])
-    back = (tall * 0.125).astype(BF)
-    row, col = picks(512, LENGTH)
-    for c in range(8):
-        inv_y_ref[:, c * 128 : c * 128 + 128] = jnp.where((row // 16) % 8 == c, back, 0.0).astype(BF)
+    back = tall * 0.125
+    row, col = picks(256, LENGTH)
+    for c in range(4):
+        block = jnp.where((row // 16) % 4 == c, back, 0.0).astype(BF)
+        inv_y_ref[:, c * 128 : c * 128 + 128] = block
     wide = tall.T
-    row, col = picks(LENGTH, 512)
-    for c in range(8):
-        block = jnp.where((col // 16) % 8 == c, wide, 0.0).astype(BF)
+    row, col = picks(LENGTH, 256)
+    for c in range(4):
+        block = jnp.where((col // 16) % 4 == c, wide, 0.0).astype(BF)
         fwd_y_ref[c * 128 : c * 128 + 128, :] = block
     place = place_ref[0]
     xr, xi = one_x_ref[place // 2, 0:1, :], one_x_ref[place // 2, 1:2, :]
@@ -307,6 +320,14 @@
     evaluate(mix(weight, modes, pattern), turned, z_ref, out_ref)
 
 
+def swapped(first, second):
+    low = lax.broadcasted_iota(jnp.int32, first.shape, 1) < 64
+    return (
+        jnp.where(low, first, pltpu.roll(second, 64, 1)),
+        jnp.where(low, pltpu.roll(first, 64, 1), second),
+    )
+
+
 def inverse(got_ref, x_ref, inv_y_ref, rows, field):
     rows[...] = got_ref[...].astype(F32)
     for g in range(4):
@@ -316,12 +337,15 @@
                 pieces = [
                     rows[pl.ds(h * 16 + g * 4 + r * 2 + z, 32, stride=32), :] for r in range(2)
                 ]
-                parts.append(jnp.concatenate(pieces, axis=0).astype(BF))
-            along = dot(x_ref[64:, :64], jnp.concatenate(parts, axis=1)).astype(BF)
-            wide = jnp.concatenate([along[:128], along[128:]], axis=1)
-            made = dot(wide, inv_y_ref[...])
-            for o in range(8):
-                field[g * 8 + o, z] = made[:, o * 128 : o * 128 + 128]
+                parts.append(jnp.concatenate(pieces, axis=0))
+            parts = jnp.concatenate(swapped(*parts), axis=1).astype(BF)
+            along = dot(x_ref[64:, :64], parts).astype(BF)
+            for quad in range(2):
+                lanes = slice(quad * 128, quad * 128 + 128)
+                wide = jnp.concatenate([along[:128, lanes], along[128:, lanes]], axis=1)
+                made = dot(wide, inv_y_ref[...])
+                for o in range(4):
+                    field[g * 8 + quad * 4 + o, z] = made[:, o * 128 : o * 128 + 128]
 
 
 def activate(value):
@@ -330,8 +354,8 @@
     return half + half * jnp.tanh(inner)
 
 
-def pointwise(block, hidden, kb_ref, bias, field):
-    bypassed = dot(kb_ref[...], hidden)
+def pointwise(block, hidden, map_ref, bias, field):
+    bypassed = dot(map_ref[...], hidden)
     made = []
     for z in range(2):
         part = field[:, z, block * 16 : block * 16 + 16, :].reshape(512, LENGTH)
@@ -341,34 +365,32 @@
 
 
 def middle_kernel(
-    got_ref, kl_ref, kb_ref, bias_ref, inv_y_ref, fwd_y_ref, x_ref, fields_hbm, hidden_hbm, out_ref,
+    got_ref, kc_ref, bias_ref, inv_y_ref, fwd_y_ref, x_ref, fields_hbm, hidden_hbm, out_ref,
     fields, rows, field, hidden, sem,
 ):
     (copy,) = fetch([(fields_hbm.at[0], fields, sem.at[0])])
     inverse(got_ref, x_ref, inv_y_ref, rows, field)
-    lift_bias = bias_ref[2]
-    lift_bias = jnp.concatenate([lift_bias, lift_bias], axis=1)
     copy.wait()
     for block in range(8):
         span = slice(block * 16, block * 16 + 16)
         raw = [fields[:, z, span, :].reshape(64, LENGTH) for z in range(2)]
-        lifted = dot(kl_ref[:, :64], jnp.concatenate(raw, axis=1)) + lift_bias
-        made = pointwise(block, lifted.astype(BF), kb_ref.at[0], bias_ref[0], field)
+        raw = jnp.concatenate(raw, axis=1)
+        made = pointwise(block, jnp.concatenate([raw, raw], axis=0), kc_ref, bias_ref[0], field)
         for z in range(2):
             hidden[:, z, span, :] = made[z].reshape(32, 16, LENGTH)
     (kept,) = fetch([(hidden, hidden_hbm, sem.at[1])])
     for g in range(4):
         for z in range(2):
-            wide = jnp.concatenate([hidden[g * 8 + c, z] for c in range(8)], axis=1)
-            along = dot(wide, fwd_y_ref[...]).astype(BF)
-            stacked = jnp.concatenate([along[:, :256], along[:, 256:]], axis=0)
-            spectrum = dot(x_ref[:64], stacked) * (1.0 / LENGTH)
-            for h in range(2):
+            stacked = []
+            for first in (g * 8, g * 8 + 4):
+                wide = jnp.concatenate([hidden[first + c, z] for c in range(4)], axis=1)
+                along = dot(wide, fwd_y_ref[...]).astype(BF)
+                stacked.append(jnp.concatenate([along[:, :128], along[:, 128:]], axis=0))
+            spectrum = dot(x_ref[:64], jnp.concatenate(stacked, axis=1)) * (1.0 / LENGTH)
+            for h, value in enumerate(swapped(spectrum[:, :128], spectrum[:, 128:])):
                 for r in range(2):
                     at = h * 16 + g * 4 + r * 2 + z
-                    rows[pl.ds(at, 32, stride=32), :] = spectrum[
-                        r * 32 : r * 32 + 32, h * 128 : h * 128 + 128
-                    ]
+                    rows[pl.ds(at, 32, stride=32), :] = value[r * 32 : r * 32 + 32]
     out_ref[...] = rows[...].astype(BF)
     kept.wait()
 
@@ -384,7 +406,7 @@
     for block in range(8):
         span = slice(block * 16, block * 16 + 16)
         raw = [hidden[:, z, span, :].reshape(512, LENGTH) for z in range(2)]
-        made = pointwise(block, jnp.concatenate(raw, axis=1), kb_ref.at[1], bias_ref[1], field)
+        made = pointwise(block, jnp.concatenate(raw, axis=1), kb_ref, bias_ref[1], field)
         for z in range(2):
             made_ref[:, z, span, :] = made[z].reshape(32, 16, LENGTH)
         kept += fetch([(made_ref.at[:, :, span, :], out_hbm.at[0, :, :, span, :], sem.at[1 + block])])
@@ -462,22 +484,25 @@
             [((4, 2, 128, 128), BF), ((64, 128), BF), ((64, 256), BF), ((128, 128), F32)],
             sems=3,
         )(fields, const["pair_y"], const["fwd_x"])
-        spectrum, spectral_weight, bypass_weight = tie((spectrum, spectral_weight, bypass_weight))
+        spectrum, spectral_weight = tie((spectrum, spectral_weight))
         spectrum = exchange(spectrum)
         weight = spectral_weight.reshape(2, 2, LENGTH, 256)
         (folded,) = call(
             fold_kernel, "fold", "ffh", [("v", (8, 64, 256), BF)], [((2, 128, 256), BF)], sems=1
         )(lift_weight, lift_bias, weight)
-        kb, kl, bias, fwd_y, inv_y, ones, z_table, x_table = call(
+        folded, bypass_weight, weight, _ = tie((folded, bypass_weight, weight, spectrum))
+        gathered = lax.all_gather(weight[1], "section", axis=0)
+        folded = exchange(folded.reshape(512, 256), "section").reshape(8, 64, 256)
+        kb, kc, bias, fwd_y, inv_y, ones, z_table, x_table = call(
             spread_kernel,
             "spread",
             "s" + "f" * 10,
             [
-                ("v", (2, 512, 512), BF),
+                ("v", (512, 512), BF),
                 ("v", (512, 128), BF),
-                ("v", (3, 512, LENGTH), F32),
-                ("v", (1024, 512), BF),
-                ("v", (512, 1024), BF),
+                ("v", (2, 512, LENGTH), F32),
+                ("v", (512, 256), BF),
+                ("v", (256, 512), BF),
                 ("v", (HALF, LENGTH), F32),
                 ("v", (2112, 128), BF),
                 ("v", (320, 256), BF),
@@ -487,11 +512,6 @@
             place, ones_x, bypass_weight, lift_weight, bypass_bias, lift_bias, const["pair_y"],
             ones_y, ones_z, const["z"], const["x"],
         )
-        later = weight[1]
-        folded, ones, later, _ = tie((folded, ones, later, spectrum))
-        folded = exchange(folded.reshape(512, 256), "section").reshape(8, 64, 256)
-        _, later = tie((folded, later))
-        gathered = lax.all_gather(later, "section", axis=0)
         (planes,) = call(
             first_mix_kernel,
             "mix0",
@@ -502,11 +522,11 @@
         hidden, spectrum = call(
             middle_kernel,
             "middle",
-            "ppppppph",
+            "pppppph",
             [("h", cube, BF), ("v", packed, BF)],
             [((4, 2, 128, 128), BF), (packed, F32), (cube, F32), (cube, BF)],
             sems=2,
-        )(exchange(planes), kl, kb, bias, inv_y, fwd_y, x_table, fields)
+        )(exchange(planes), kc, bias, inv_y, fwd_y, x_table, fields)
         (planes,) = call(
             mix_kernel,
             "mix1",

time: 142 us -> 132 us (0.930)
  blocking collectives: 80.5 us -> 54.9 us
  waiting for transfers between devices: 0.02 us -> 13 us
  starting transfers between devices: 11.9 us -> 21.7 us
  local copies, waits for them, and re-layouts: 9.81 us -> 3.28 us
    all_to_all x4 -> x3, blocking collectives: 80.5 us -> 54.9 us  [exchange(): return lax.all_to_all(value, axis, split_axis=0, concat_axis=0, tiled=True)]
    all_to_all x1 -> x2, waiting for transfers between devices: 0.01 us -> 13 us  [exchange(): return lax.all_to_all(value, axis, split_axis=0, concat_axis=0, tiled=True)]
    all_to_all x1 -> x2, starting transfers between devices: 11.8 us -> 21.7 us  [exchange(): return lax.all_to_all(value, axis, split_axis=0, concat_axis=0, tiled=True)]
    unnamed x20 -> x0, local copies, waits for them, and re-layouts: 6.45 us -> none
  transfers between devices with their start and end apart: 2 -> 3, of which waited for: 0 -> 2; matrix products, arithmetic and copies ran while one was open for 2% -> 1% of each run, Pallas kernels for 10% -> 11%
where the time goes in v2:
time: 132 us; the launch traced here: 131 us
  blocking collectives  54.9 us (42%)
  Pallas kernels  24.7 us (19%)
  starting transfers between devices  21.7 us (16%)
  between operations  13.5 us (10%)
  waiting for transfers between devices  13 us (10%)
  local copies, waits for them, and re-layouts  3.28 us (2%)
    all_to_all x3, blocking collectives, exchange(): return lax.all_to_all(value, axis, split_axis=0, concat_axis=0, tiled=True)  54.9 us
    pallas_call x7, Pallas kernels, run(): pl.pallas_call(body, name=name, out_shape=[spaces[letter](shape, kind) fo...  24.7 us
    all_to_all x2, starting transfers between devices, exchange(): return lax.all_to_all(value, axis, split_axis=0, concat_axis=0, tiled=True)  21.7 us
    all_to_all x2, waiting for transfers between devices, exchange(): return lax.all_to_all(value, axis, split_axis=0, concat_axis=0, tiled=True)  13 us
  transfers between devices with their start and end apart: 3, of which 2 were waited for; matrix products, arithmetic and copies ran while one was open for 1% of the time, Pallas kernels for 11%

profile of v2, /device:TPU:1, one launch (start us, length us, event | category | flops | bytes accessed | tf_op | source)
XLA Modules:
  0.0 131.0 jit_solution(11414513518842986720)
XLA Ops:
  6.5 2.3 %start.1 = bf16[128,128]{1,0:T(8,128)(2,1)} custom-call(bf16[1,4,2,128,128]{4,3,2,1,0:T(8,128)(2,1)} %refs_6_.2, bf16[64,128]{1,0:T(8,128)(2,1)} %constant.18.clone.refs_1_.refs_6_, bf16[64,256]{1,0:T(8,128)(2,1)} %constant.19.clone.refs_2_), custom_call_target="tpu_custom_call" | custom-call | tf_op jit(solution)/shard_map/start/pallas_call | solution.py:447
  8.8 11.6 %all-to-all-start = ((bf16[64,2,128]{2,1,0:T(2,128)(2,1)}), bf16[64,2,128]{2,1,0:T(2,128)(2,1)S(1)}, u32[]{:S(2)}, u32[]{:S(2)}) async-start(bf16[64,2,128]{2,1,0:T(2,128)(2,1)} %bitcast.1), calls=%async_computation | async-start | bytes 65536 | tf_op jit(solution)/shard_map/all_to_all | solution.py:461
  20.4 0.0 all-gather.2.cloned.1.call-start
  20.5 1.7 %reshape.21.refs_2_ = bf16[2,2,128,256]{3,2,1,0:T(8,128)(2,1)} reshape(bf16[2,2,32,4,256]{4,3,2,1,0:T(4,128)(2,1)} %param.16) | data formatting | bytes 524288 | tf_op jit(solution)/shard_map/reshape | solution.py:489
  22.2 2.5 %fold.1 = bf16[8,64,256]{2,1,0:T(8,128)(2,1)} custom-call(bf16[4,32]{1,0:T(4,128)(2,1)} %refs_3_.1, bf16[1,32]{1,0:T(2,128)(2,1)} %bitcast.17, bf16[2,2,128,256]{3,2,1,0:T(8,128)(2,1)} %reshape.21.refs_2_), custom_call_target="tpu_custom_call" | custom-call | tf_op jit(solution)/shard_map/fold/pallas_call | solution.py:447
  24.7 5.0 %all-to-all-done = bf16[64,2,128]{2,1,0:T(2,128)(2,1)S(1)} async-done(((bf16[64,2,128]{2,1,0:T(2,128)(2,1)}), bf16[64,2,128]{2,1,0:T(2,128)(2,1)S(1)}, u32[]{:S(2)}, u32[]{:S(2)}) %all-to-all-start) | async-done | bytes 32800 | tf_op jit(solution)/shard_map/all_to_all | solution.py:461
  29.7 1.6 %slice.3 = bf16[1,2,128,256]{3,2,1,0:T(8,128)(2,1)} slice(bf16[2,2,128,256]{3,2,1,0:T(8,128)(2,1)} %reshape.21.refs_2_), slice={[1:2], [0:2], [0:128], [0:256]} | slice | bytes 262144 | tf_op jit(solution)/shard_map/slice | solution.py:494
  31.3 0.0 all-gather.2.cloned.1.call-update
  31.3 10.0 %all-to-all-start.1 = ((bf16[8,64,256]{2,1,0:T(8,128)(2,1)}), bf16[8,64,256]{2,1,0:T(8,128)(2,1)S(1)}, u32[]{:S(2)}, u32[]{:S(2)}) async-start(bf16[8,64,256]{2,1,0:T(8,128)(2,1)} %fold.1), calls=%async_computation.1 | async-start | bytes 524288 | tf_op jit(solution)/shard_map/all_to_all | solution.py:461
  41.4 2.8 %spread.1 = (bf16[512,512]{1,0:T(8,128)(2,1)S(1)}, bf16[512,128]{1,0:T(8,128)(2,1)S(1)}, f32[2,512,128]{2,1,0:T(8,128)S(1)}, bf16[512,256]{1,0:T(8,128)(2,1)S(1)...) custom-call(s32[1]{0:T(128)} %bitcast.refs_0_, ...), custom_call_target="tpu_custom_call" | custom-call | tf_op jit(solution)/shard_map/spread/pallas_call | solution.py:447
  44.2 7.9 %all-to-all-done.1.refs_2_ = bf16[8,64,256]{2,1,0:T(8,128)(2,1)S(1)} async-done(((bf16[8,64,256]{2,1,0:T(8,128)(2,1)}), bf16[8,64,256]{2,1,0:T(8,128)(2,1)S(1)}, u32[]{:S(2)}, u32[]{:S(2)}) %all-to-all-start.1) | async-done | bytes 262176 | tf_op jit(solution)/shard_map/all_to_all | solution.py:461
  52.1 0.9 mix0.1
  53.1 19.1 %all_to_all.50 = bf16[64,16,128]{2,1,0:T(8,128)(2,1)S(1)} all-to-all(bf16[64,16,128]{2,1,0:T(8,128)(2,1)S(1)} %bitcast.14), channel_id=1, replica_groups=mesh['section'=8,'slab'=64] {'slab'}, dimensions={0} | all-to-all | bytes 524288 | tf_op jit(solution)/shard_map/all_to_all | solution.py:461
  72.2 7.8 %middle.1 = (bf16[32,2,128,128]{3,2,1,0:T(8,128)(2,1)}, bf16[1024,128]{1,0:T(8,128)(2,1)S(1)}) custom-call(bf16[1024,128]{1,0:T(8,128)(2,1)S(1)} %bitcast.12, bf16[512,128]{1,0:T(8,128)(2,1)S(1)} %get-tuple-element.26.refs_1_, f32[2,512,128]{2,1,0:T(8,128)S(1)} %get-tuple-element.27.refs_2_, bf16[256,512]{1,0:T(8,128)(2,1)S(1)} %get-tuple-element.28.refs_3_, ...), custom_call_target="tpu_custom_call" | custom-call | tf_op jit(solution)/shard_map/middle/pallas_call | solution.py:447
  80.0 17.9 %all_to_all.51 = bf16[64,16,128]{2,1,0:T(8,128)(2,1)S(1)} all-to-all(bf16[64,16,128]{2,1,0:T(8,128)(2,1)S(1)} %bitcast.15), channel_id=1, replica_groups=mesh['section'=8,'slab'=64] {'slab'}, dimensions={0} | all-to-all | bytes 524288 | tf_op jit(solution)/shard_map/all_to_all | solution.py:461
  97.9 0.0 all-gather.2.cloned.1.call-done.refs_3_
  97.9 2.0 %mix1.1 = bf16[1024,128]{1,0:T(8,128)(2,1)S(1)} custom-call(s32[1]{0:T(128)} %bitcast.refs_0_, bf16[1024,128]{1,0:T(8,128)(2,1)S(1)} %bitcast.10, bf16[2112,128]{1,0:T(8,128)(2,1)S(1)} %get-tuple-element.25.refs_4_.refs_2_, bf16[8,2,128,256]{3,2,1,0:T(8,128)(2,1)} %all-gather.2.cloned.1.call-done.refs_3_), custom_call_target="tpu_custom_call" | custom-call | tf_op jit(solution)/shard_map/mix1/pallas_call | solution.py:447
  99.9 17.8 %all_to_all.52 = bf16[64,16,128]{2,1,0:T(8,128)(2,1)S(1)} all-to-all(bf16[64,16,128]{2,1,0:T(8,128)(2,1)S(1)} %bitcast.13), channel_id=1, replica_groups=mesh['section'=8,'slab'=64] {'slab'}, dimensions={0} | all-to-all | bytes 524288 | tf_op jit(solution)/shard_map/all_to_all | solution.py:461
  117.7 6.4 %last.1 = bf16[1,32,2,128,128]{4,3,2,1,0:T(8,128)(2,1)} custom-call(bf16[1024,128]{1,0:T(8,128)(2,1)S(1)} %bitcast.11, bf16[512,512]{1,0:T(8,128)(2,1)S(1)} %get-tuple-element.33.refs_1_, f32[2,512,128]{2,1,0:T(8,128)S(1)} %get-tuple-element.27.refs_2_, bf16[256,512]{1,0:T(8,128)(2,1)S(1)} %get-tuple-element.28.refs_3_, ...), custom_call_target="tpu_custom_call" | custom-call | tf_op jit(solution)/shard_map/last/pallas_call | solution.py:447
Async XLA Ops:
  8.8 20.9 %all-to-all-start = ((bf16[64,2,128]{2,1,0:T(2,128)(2,1)}), bf16[64,2,128]{2,1,0:T(2,128)(2,1)S(1)}, u32[]{:S(2)}, u32[]{:S(2)}) async-start(bf16[64,2,128]{2,1,0:T(2,128)(2,1)} %bitcast.1), calls=%async_computation | async-start | bytes 65536 | tf_op jit(solution)/shard_map/all_to_all | solution.py:461
  20.4 77.4 %all-gather.2.cloned.1.call-start = ((), (), s32[]{:S(2)}) async-start(), calls=%async_computation.5 | async-start | bytes 1179648 | tf_op jit(solution)/shard_map/all_gather | solution.py:494
  31.3 20.8 %all-to-all-start.1 = ((bf16[8,64,256]{2,1,0:T(8,128)(2,1)}), bf16[8,64,256]{2,1,0:T(8,128)(2,1)S(1)}, u32[]{:S(2)}, u32[]{:S(2)}) async-start(bf16[8,64,256]{2,1,0:T(8,128)(2,1)} %fold.1), calls=%async_computation.1 | async-start | bytes 524288 | tf_op jit(solution)/shard_map/all_to_all | solution.py:461
Sparse Core Ops, SparseCore 0:
  31.4 38.3 all-gather.1

commit v3 on v2

--- a/solution.py
+++ b/solution.py
@@ -13,6 +13,8 @@
 HALF = 2 * K
 LENGTH = 128
 SLABS = 64
+UNROLL_A = 4
+UNROLL_B = 8
 BF = jnp.bfloat16
 F32 = jnp.float32
 
@@ -143,8 +145,10 @@
     ones_ref[...] = jnp.concatenate([zr * pr - zi * pi, zr * pi + zi * pr], axis=0)
 
 
-def fold_kernel(lift_ref, lift_bias_ref, weight_hbm, out_ref, weight, sem):
-    (copy,) = fetch([(weight_hbm.at[0], weight, sem.at[0])])
+def fold_kernel(lift_ref, lift_bias_ref, weight_hbm, out_ref, later_hbm, weight, sem):
+    copy, kept = fetch(
+        [(weight_hbm.at[0], weight, sem.at[0]), (weight_hbm.at[1], later_hbm, sem.at[1])]
+    )
     row, col = picks(HALF, 4)
     pick = one_hot((row % 8 == col))
     row, col = picks(HALF, HALF)
@@ -157,6 +161,7 @@
         folded = dot(lift, weight[r]).astype(BF)
         for section in range(8):
             out_ref[section, r * HALF : r * HALF + HALF, :] = folded
+    kept.wait()
 
 
 def start_kernel(fields_hbm, pair_y_hbm, fwd_x_hbm, out_ref, fields, pair_y, fwd_x, rows, sem):
@@ -330,22 +335,24 @@
 
 def inverse(got_ref, x_ref, inv_y_ref, rows, field):
     rows[...] = got_ref[...].astype(F32)
-    for g in range(4):
-        for z in range(2):
-            parts = []
-            for h in range(2):
-                pieces = [
-                    rows[pl.ds(h * 16 + g * 4 + r * 2 + z, 32, stride=32), :] for r in range(2)
-                ]
-                parts.append(jnp.concatenate(pieces, axis=0))
-            parts = jnp.concatenate(swapped(*parts), axis=1).astype(BF)
-            along = dot(x_ref[64:, :64], parts).astype(BF)
-            for quad in range(2):
-                lanes = slice(quad * 128, quad * 128 + 128)
-                wide = jnp.concatenate([along[:128, lanes], along[128:, lanes]], axis=1)
-                made = dot(wide, inv_y_ref[...])
-                for o in range(4):
-                    field[g * 8 + quad * 4 + o, z] = made[:, o * 128 : o * 128 + 128]
+
+    def step(index, carry):
+        g, z = index // 2, index % 2
+        parts = []
+        for h in range(2):
+            pieces = [rows[pl.ds(h * 16 + g * 4 + r * 2 + z, 32, stride=32), :] for r in range(2)]
+            parts.append(jnp.concatenate(pieces, axis=0))
+        parts = jnp.concatenate(swapped(*parts), axis=1).astype(BF)
+        along = dot(x_ref[64:, :64], parts).astype(BF)
+        for quad in range(2):
+            lanes = slice(quad * 128, quad * 128 + 128)
+            wide = jnp.concatenate([along[:128, lanes], along[128:, lanes]], axis=1)
+            made = dot(wide, inv_y_ref[...])
+            for o in range(4):
+                field[g * 8 + quad * 4 + o, z] = made[:, o * 128 : o * 128 + 128]
+        return carry
+
+    lax.fori_loop(0, 8, step, 0, unroll=UNROLL_A)
 
 
 def activate(value):
@@ -354,11 +361,11 @@
     return half + half * jnp.tanh(inner)
 
 
-def pointwise(block, hidden, map_ref, bias, field):
+def pointwise(span, hidden, map_ref, bias, field):
     bypassed = dot(map_ref[...], hidden)
     made = []
     for z in range(2):
-        part = field[:, z, block * 16 : block * 16 + 16, :].reshape(512, LENGTH)
+        part = field[:, z, span, :].reshape(512, LENGTH)
         value = bypassed[:, z * 128 : z * 128 + 128] + bias + part
         made.append(activate(value).astype(BF))
     return made
@@ -371,26 +378,32 @@
     (copy,) = fetch([(fields_hbm.at[0], fields, sem.at[0])])
     inverse(got_ref, x_ref, inv_y_ref, rows, field)
     copy.wait()
-    for block in range(8):
-        span = slice(block * 16, block * 16 + 16)
+    def apply(block, carry):
+        span = pl.ds(pl.multiple_of(block * 16, 16), 16)
         raw = [fields[:, z, span, :].reshape(64, LENGTH) for z in range(2)]
         raw = jnp.concatenate(raw, axis=1)
-        made = pointwise(block, jnp.concatenate([raw, raw], axis=0), kc_ref, bias_ref[0], field)
+        made = pointwise(span, jnp.concatenate([raw, raw], axis=0), kc_ref, bias_ref[0], field)
         for z in range(2):
             hidden[:, z, span, :] = made[z].reshape(32, 16, LENGTH)
+        return carry
+
+    lax.fori_loop(0, 8, apply, 0, unroll=UNROLL_B)
     (kept,) = fetch([(hidden, hidden_hbm, sem.at[1])])
-    for g in range(4):
-        for z in range(2):
-            stacked = []
-            for first in (g * 8, g * 8 + 4):
-                wide = jnp.concatenate([hidden[first + c, z] for c in range(4)], axis=1)
-                along = dot(wide, fwd_y_ref[...]).astype(BF)
-                stacked.append(jnp.concatenate([along[:, :128], along[:, 128:]], axis=0))
-            spectrum = dot(x_ref[:64], jnp.concatenate(stacked, axis=1)) * (1.0 / LENGTH)
-            for h, value in enumerate(swapped(spectrum[:, :128], spectrum[:, 128:])):
-                for r in range(2):
-                    at = h * 16 + g * 4 + r * 2 + z
-                    rows[pl.ds(at, 32, stride=32), :] = value[r * 32 : r * 32 + 32]
+    def forward(index, carry):
+        g, z = index // 2, index % 2
+        stacked = []
+        for quad in range(2):
+            wide = jnp.concatenate([hidden[g * 8 + quad * 4 + c, z] for c in range(4)], axis=1)
+            along = dot(wide, fwd_y_ref[...]).astype(BF)
+            stacked.append(jnp.concatenate([along[:, :128], along[:, 128:]], axis=0))
+        spectrum = dot(x_ref[:64], jnp.concatenate(stacked, axis=1)) * (1.0 / LENGTH)
+        for h, value in enumerate(swapped(spectrum[:, :128], spectrum[:, 128:])):
+            for r in range(2):
+                at = h * 16 + g * 4 + r * 2 + z
+                rows[pl.ds(at, 32, stride=32), :] = value[r * 32 : r * 32 + 32]
+        return carry
+
+    lax.fori_loop(0, 8, forward, 0, unroll=UNROLL_A)
     out_ref[...] = rows[...].astype(BF)
     kept.wait()
 
@@ -402,16 +415,24 @@
     (copy,) = fetch([(hidden_hbm, hidden, sem.at[0])])
     inverse(got_ref, x_ref, inv_y_ref, rows, field)
     copy.wait()
-    kept = []
-    for block in range(8):
-        span = slice(block * 16, block * 16 + 16)
+
+    def keep(block):
+        span = pl.ds(pl.multiple_of(block * 16, 16), 16)
+        source, target = made_ref.at[:, :, span, :], out_hbm.at[0, :, :, span, :]
+        return pltpu.make_async_copy(source, target, sem.at[1 + block])
+
+    def apply(block, carry):
+        span = pl.ds(pl.multiple_of(block * 16, 16), 16)
         raw = [hidden[:, z, span, :].reshape(512, LENGTH) for z in range(2)]
-        made = pointwise(block, jnp.concatenate(raw, axis=1), kb_ref, bias_ref[1], field)
+        made = pointwise(span, jnp.concatenate(raw, axis=1), kb_ref, bias_ref[1], field)
         for z in range(2):
             made_ref[:, z, span, :] = made[z].reshape(32, 16, LENGTH)
-        kept += fetch([(made_ref.at[:, :, span, :], out_hbm.at[0, :, :, span, :], sem.at[1 + block])])
-    for copy in kept:
-        copy.wait()
+        keep(block).start()
+        return carry
+
+    lax.fori_loop(0, 8, apply, 0, unroll=UNROLL_B)
+    for block in range(8):
+        keep(block).wait()
 
 
 def call(kernel, name, inputs, outputs, scratch, sems=0, limit=24):
@@ -487,11 +508,16 @@
         spectrum, spectral_weight = tie((spectrum, spectral_weight))
         spectrum = exchange(spectrum)
         weight = spectral_weight.reshape(2, 2, LENGTH, 256)
-        (folded,) = call(
-            fold_kernel, "fold", "ffh", [("v", (8, 64, 256), BF)], [((2, 128, 256), BF)], sems=1
+        folded, later = call(
+            fold_kernel,
+            "fold",
+            "ffh",
+            [("v", (8, 64, 256), BF), ("h", (2, LENGTH, 256), BF)],
+            [((2, 128, 256), BF)],
+            sems=2,
         )(lift_weight, lift_bias, weight)
-        folded, bypass_weight, weight, _ = tie((folded, bypass_weight, weight, spectrum))
-        gathered = lax.all_gather(weight[1], "section", axis=0)
+        folded, bypass_weight, later, _ = tie((folded, bypass_weight, later, spectrum))
+        gathered = lax.all_gather(later, "section", axis=0)
         folded = exchange(folded.reshape(512, 256), "section").reshape(8, 64, 256)
         kb, kc, bias, fwd_y, inv_y, ones, z_table, x_table = call(
             spread_kernel,

time: 132 us -> 131 us (level)
  waiting for transfers between devices: 13 us -> 8.65 us
  blocking collectives: 54.9 us -> 58.8 us
  Pallas kernels: 24.7 us -> 26.3 us
  local copies, waits for them, and re-layouts: 3.28 us -> 1.72 us
    all_to_all x2, waiting for transfers between devices: 13 us -> 8.63 us  [exchange(): return lax.all_to_all(value, axis, split_axis=0, concat_axis=0, tiled=True)]
    all_to_all x3, blocking collectives: 54.9 us -> 58.8 us  [exchange(): return lax.all_to_all(value, axis, split_axis=0, concat_axis=0, tiled=True)]
    pallas_call x7, Pallas kernels: 24.7 us -> 26.3 us  [run(): pl.pallas_call(body, name=name, out_shape=[spaces[letter](shape, kind) fo...]
    slice x1 -> x0, local copies, waits for them, and re-layouts: 1.56 us -> none  [on_device(): gathered = lax.all_gather(weight[1], 'section', axis=0)]
  transfers between devices with their start and end apart: 3 -> 3, of which waited for: 2 -> 2; matrix products, arithmetic and copies ran while one was open for 1% -> 1% of each run, Pallas kernels for 11% -> 13%
where the time goes in v3:
time: 131 us
  blocking collectives  58.8 us (45%)
  Pallas kernels  26.3 us (20%)
  starting transfers between devices  21.7 us (17%)
  between operations  13.5 us (10%)
  waiting for transfers between devices  8.65 us (7%)
  local copies, waits for them, and re-layouts  1.72 us (1%)
    all_to_all x3, blocking collectives, exchange(): return lax.all_to_all(value, axis, split_axis=0, concat_axis=0, tiled=True)  58.8 us
    pallas_call x7, Pallas kernels, run(): pl.pallas_call(body, name=name, out_shape=[spaces[letter](shape, kind) fo...  26.3 us
    all_to_all x2, starting transfers between devices, exchange(): return lax.all_to_all(value, axis, split_axis=0, concat_axis=0, tiled=True)  21.7 us
    all_to_all x2, waiting for transfers between devices, exchange(): return lax.all_to_all(value, axis, split_axis=0, concat_axis=0, tiled=True)  8.63 us
  transfers between devices with their start and end apart: 3, of which 2 were waited for; matrix products, arithmetic and copies ran while one was open for 1% of the time, Pallas kernels for 13%

profile of v3, /device:TPU:1, one launch (start us, length us, event | category | flops | bytes accessed | tf_op | source)
XLA Modules:
  0.0 130.6 jit_solution(12398118448091500146)
XLA Ops:
  6.5 2.2 %start.1 = bf16[128,128]{1,0:T(8,128)(2,1)} custom-call(bf16[1,4,2,128,128]{4,3,2,1,0:T(8,128)(2,1)} %refs_6_.2, bf16[64,128]{1,0:T(8,128)(2,1)} %constant.18.clone.refs_1_.refs_6_, bf16[64,256]{1,0:T(8,128)(2,1)} %constant.19.clone.refs_2_), custom_call_target="tpu_custom_call" | custom-call | tf_op jit(solution)/shard_map/start/pallas_call | solution.py:468
  8.8 11.6 %all-to-all-start = ((bf16[64,2,128]{2,1,0:T(2,128)(2,1)}), bf16[64,2,128]{2,1,0:T(2,128)(2,1)S(1)}, u32[]{:S(2)}, u32[]{:S(2)}) async-start(bf16[64,2,128]{2,1,0:T(2,128)(2,1)} %bitcast.1), calls=%async_computation | async-start | bytes 65536 | tf_op jit(solution)/shard_map/all_to_all | solution.py:482
  20.4 0.0 all-gather.3.cloned.1.call-start
  20.5 1.7 %reshape.21.refs_2_ = bf16[2,2,128,256]{3,2,1,0:T(8,128)(2,1)} reshape(bf16[2,2,32,4,256]{4,3,2,1,0:T(4,128)(2,1)} %param.16) | data formatting | bytes 524288 | tf_op jit(solution)/shard_map/reshape | solution.py:510
  22.2 6.5 %fold.1 = (bf16[8,64,256]{2,1,0:T(8,128)(2,1)}, bf16[2,128,256]{2,1,0:T(8,128)(2,1)}) custom-call(bf16[4,32]{1,0:T(4,128)(2,1)} %refs_3_.1, bf16[1,32]{1,0:T(2,128)(2,1)} %bitcast.19, bf16[2,2,128,256]{3,2,1,0:T(8,128)(2,1)} %reshape.21.refs_2_), custom_call_target="tpu_custom_call" | custom-call | tf_op jit(solution)/shard_map/fold/pallas_call | solution.py:468
  28.7 1.0 all-to-all-done
  29.7 0.0 all-gather.3.cloned.1.call-update
  29.7 10.1 %all-to-all-start.1 = ((bf16[8,64,256]{2,1,0:T(8,128)(2,1)}), bf16[8,64,256]{2,1,0:T(8,128)(2,1)S(1)}, u32[]{:S(2)}, u32[]{:S(2)}) async-start(bf16[8,64,256]{2,1,0:T(8,128)(2,1)} %get-tuple-element.26), calls=%async_computation.1 | async-start | bytes 524288 | tf_op jit(solution)/shard_map/all_to_all | solution.py:482
  39.8 2.8 %spread.1 = (bf16[512,512]{1,0:T(8,128)(2,1)S(1)}, bf16[512,128]{1,0:T(8,128)(2,1)S(1)}, f32[2,512,128]{2,1,0:T(8,128)S(1)}, bf16[512,256]{1,0:T(8,128)(2,1)S(1)...) custom-call(s32[1]{0:T(128)} %bitcast.refs_0_, ...), custom_call_target="tpu_custom_call" | custom-call | tf_op jit(solution)/shard_map/spread/pallas_call | solution.py:468
  42.6 7.6 %all-to-all-done.1.refs_2_ = bf16[8,64,256]{2,1,0:T(8,128)(2,1)S(1)} async-done(((bf16[8,64,256]{2,1,0:T(8,128)(2,1)}), bf16[8,64,256]{2,1,0:T(8,128)(2,1)S(1)}, u32[]{:S(2)}, u32[]{:S(2)}) %all-to-all-start.1) | async-done | bytes 262176 | tf_op jit(solution)/shard_map/all_to_all | solution.py:482
  50.2 0.9 mix0.1
  51.2 23.1 %all_to_all.50 = bf16[64,16,128]{2,1,0:T(8,128)(2,1)S(1)} all-to-all(bf16[64,16,128]{2,1,0:T(8,128)(2,1)S(1)} %bitcast.15), channel_id=1, replica_groups=mesh['section'=8,'slab'=64] {'slab'}, dimensions={0} | all-to-all | bytes 524288 | tf_op jit(solution)/shard_map/all_to_all | solution.py:482
  74.3 6.5 %middle.1 = (bf16[32,2,128,128]{3,2,1,0:T(8,128)(2,1)}, bf16[1024,128]{1,0:T(8,128)(2,1)S(1)}) custom-call(bf16[1024,128]{1,0:T(8,128)(2,1)S(1)} %bitcast.13, bf16[512,128]{1,0:T(8,128)(2,1)S(1)} %get-tuple-element.30.refs_1_, f32[2,512,128]{2,1,0:T(8,128)S(1)} %get-tuple-element.31.refs_2_, bf16[256,512]{1,0:T(8,128)(2,1)S(1)} %get-tuple-element.32.refs_3_, ...), custom_call_target="tpu_custom_call" | custom-call | tf_op jit(solution)/shard_map/middle/pallas_call | solution.py:468
  80.8 17.8 %all_to_all.51 = bf16[64,16,128]{2,1,0:T(8,128)(2,1)S(1)} all-to-all(bf16[64,16,128]{2,1,0:T(8,128)(2,1)S(1)} %bitcast.16), channel_id=1, replica_groups=mesh['section'=8,'slab'=64] {'slab'}, dimensions={0} | all-to-all | bytes 524288 | tf_op jit(solution)/shard_map/all_to_all | solution.py:482
  98.7 0.0 all-gather.3.cloned.1.call-done
  98.7 2.0 %mix1.1 = bf16[1024,128]{1,0:T(8,128)(2,1)S(1)} custom-call(s32[1]{0:T(128)} %bitcast.refs_0_, bf16[1024,128]{1,0:T(8,128)(2,1)S(1)} %bitcast.11, bf16[2112,128]{1,0:T(8,128)(2,1)S(1)} %get-tuple-element.29.refs_4_.refs_2_, bf16[8,2,128,256]{3,2,1,0:T(8,128)(2,1)} %bitcast.18), custom_call_target="tpu_custom_call" | custom-call | tf_op jit(solution)/shard_map/mix1/pallas_call | solution.py:468
  100.7 17.8 %all_to_all.52 = bf16[64,16,128]{2,1,0:T(8,128)(2,1)S(1)} all-to-all(bf16[64,16,128]{2,1,0:T(8,128)(2,1)S(1)} %bitcast.14), channel_id=1, replica_groups=mesh['section'=8,'slab'=64] {'slab'}, dimensions={0} | all-to-all | bytes 524288 | tf_op jit(solution)/shard_map/all_to_all | solution.py:482
  118.5 5.3 %last.1 = bf16[1,32,2,128,128]{4,3,2,1,0:T(8,128)(2,1)} custom-call(bf16[1024,128]{1,0:T(8,128)(2,1)S(1)} %bitcast.12, bf16[512,512]{1,0:T(8,128)(2,1)S(1)} %get-tuple-element.37.refs_1_, f32[2,512,128]{2,1,0:T(8,128)S(1)} %get-tuple-element.31.refs_2_, bf16[256,512]{1,0:T(8,128)(2,1)S(1)} %get-tuple-element.32.refs_3_, ...), custom_call_target="tpu_custom_call" | custom-call | tf_op jit(solution)/shard_map/last/pallas_call | solution.py:468
Async XLA Ops:
  8.8 20.9 %all-to-all-start = ((bf16[64,2,128]{2,1,0:T(2,128)(2,1)}), bf16[64,2,128]{2,1,0:T(2,128)(2,1)S(1)}, u32[]{:S(2)}, u32[]{:S(2)}) async-start(bf16[64,2,128]{2,1,0:T(2,128)(2,1)} %bitcast.1), calls=%async_computation | async-start | bytes 65536 | tf_op jit(solution)/shard_map/all_to_all | solution.py:482
  20.4 78.2 %all-gather.3.cloned.1.call-start = ((), (), s32[]{:S(2)}) async-start(), calls=%async_computation.5 | async-start | bytes 1179648 | tf_op jit(solution)/shard_map/all_gather | solution.py:520
  29.7 20.5 %all-to-all-start.1 = ((bf16[8,64,256]{2,1,0:T(8,128)(2,1)}), bf16[8,64,256]{2,1,0:T(8,128)(2,1)S(1)}, u32[]{:S(2)}, u32[]{:S(2)}) async-start(bf16[8,64,256]{2,1,0:T(8,128)(2,1)} %get-tuple-element.26), calls=%async_computation.1 | async-start | bytes 524288 | tf_op jit(solution)/shard_map/all_to_all | solution.py:482
Sparse Core Ops, SparseCore 0:
  29.9 40.7 all-gather.2

commit v4 on v3

--- a/solution.py
+++ b/solution.py
@@ -145,10 +145,8 @@
     ones_ref[...] = jnp.concatenate([zr * pr - zi * pi, zr * pi + zi * pr], axis=0)
 
 
-def fold_kernel(lift_ref, lift_bias_ref, weight_hbm, out_ref, later_hbm, weight, sem):
-    copy, kept = fetch(
-        [(weight_hbm.at[0], weight, sem.at[0]), (weight_hbm.at[1], later_hbm, sem.at[1])]
-    )
+def fold_kernel(lift_ref, lift_bias_ref, weight_hbm, out_ref, later_hbm, weight, later, sem):
+    copy, passed = fetch([(weight_hbm.at[0], weight, sem.at[0]), (weight_hbm.at[1], later, sem.at[1])])
     row, col = picks(HALF, 4)
     pick = one_hot((row % 8 == col))
     row, col = picks(HALF, HALF)
@@ -156,6 +154,8 @@
     row, col = picks(HALF, LENGTH)
     lift = dot(lift.astype(BF), one_hot(row == col // 4))
     lift = jnp.where(row // 8 == col % 4, lift, 0.0).astype(BF)
+    passed.wait()
+    (kept,) = fetch([(later, later_hbm, sem.at[2])])
     copy.wait()
     for r in range(2):
         folded = dot(lift, weight[r]).astype(BF)
@@ -197,7 +197,7 @@
     out_ref[...] = rows[...].astype(BF)
 
 
-def mix(weight_ref, modes, pattern):
+def mix(weight_ref, modes, pattern, copies):
     low = lax.broadcasted_iota(jnp.int32, (8, LENGTH), 0) < 4
     for pair in range(16):
         for r in range(2):
@@ -207,6 +207,7 @@
                 pattern[pair, r, half] = jnp.where(low, even, odd)
     mixed = {}
     for g in range(4):
+        copies[g].wait()
         total = {}
         for side in range(2):
             section = 2 * g + side
@@ -311,7 +312,7 @@
 def mix_kernel(
     place_ref, got_ref, z_ref, weight_hbm, out_ref, weight, turned, modes, pattern, sem
 ):
-    (copy,) = fetch([(weight_hbm, weight, sem.at[0])])
+    copies = fetch([(weight_hbm.at[pl.ds(2 * g, 2)], weight.at[pl.ds(2 * g, 2)], sem.at[g]) for g in range(4)])
     value = None
     for block in range(8):
         span = slice(block * 128, block * 128 + 128)
@@ -321,8 +322,7 @@
     value = jnp.where(dropped(place_ref, value.shape), 0.0, value)
     turned[...] = value.T
     unravel(turned, 4, modes)
-    copy.wait()
-    evaluate(mix(weight, modes, pattern), turned, z_ref, out_ref)
+    evaluate(mix(weight, modes, pattern, copies), turned, z_ref, out_ref)
 
 
 def swapped(first, second):
@@ -513,8 +513,8 @@
             "fold",
             "ffh",
             [("v", (8, 64, 256), BF), ("h", (2, LENGTH, 256), BF)],
-            [((2, 128, 256), BF)],
-            sems=2,
+            [((2, 128, 256), BF), ((2, 128, 256), BF)],
+            sems=3,
         )(lift_weight, lift_bias, weight)
         folded, bypass_weight, later, _ = tie((folded, bypass_weight, later, spectrum))
         gathered = lax.all_gather(later, "section", axis=0)
@@ -562,7 +562,7 @@
                 ((8, 2, 128, 256), BF), ((128, 128), F32), ((2, 2, 32, 128), F32),
                 ((16, 2, 2, 8, 128), F32),
             ],
-            sems=1,
+            sems=4,
         )(place, exchange(spectrum), z_table, gathered)
         (features,) = call(
             last_kernel,

time: 131 us -> 127 us (0.969)
  Pallas kernels: 26.3 us -> 22.6 us
  blocking collectives: 58.8 us -> 55.3 us
  waiting for transfers between devices: 8.65 us -> 12.1 us
    pallas_call x7, Pallas kernels: 26.3 us -> 22.6 us  [run(): pl.pallas_call(body, name=name, out_shape=[spaces[letter](shape, kind) fo...]
    all_to_all x3, blocking collectives: 58.8 us -> 55.3 us  [exchange(): return lax.all_to_all(value, axis, split_axis=0, concat_axis=0, tiled=True)]
    all_to_all x2, waiting for transfers between devices: 8.63 us -> 12.1 us  [exchange(): return lax.all_to_all(value, axis, split_axis=0, concat_axis=0, tiled=True)]
  transfers between devices with their start and end apart: 3 -> 3, of which waited for: 2 -> 2; matrix products, arithmetic and copies ran while one was open for 1% -> 1% of each run, Pallas kernels for 13% -> 11%
where the time goes in v4:
time: 127 us
  blocking collectives  55.3 us (44%)
  Pallas kernels  22.6 us (18%)
  starting transfers between devices  21.7 us (17%)
  between operations  13.5 us (11%)
  waiting for transfers between devices  12.1 us (10%)
  local copies, waits for them, and re-layouts  1.72 us (1%)
    all_to_all x3, blocking collectives, exchange(): return lax.all_to_all(value, axis, split_axis=0, concat_axis=0, tiled=True)  55.3 us
    pallas_call x7, Pallas kernels, run(): pl.pallas_call(body, name=name, out_shape=[spaces[letter](shape, kind) fo...  22.6 us
    all_to_all x2, starting transfers between devices, exchange(): return lax.all_to_all(value, axis, split_axis=0, concat_axis=0, tiled=True)  21.7 us
    all_to_all x2, waiting for transfers between devices, exchange(): return lax.all_to_all(value, axis, split_axis=0, concat_axis=0, tiled=True)  12.1 us
  transfers between devices with their start and end apart: 3, of which 2 were waited for; matrix products, arithmetic and copies ran while one was open for 1% of the time, Pallas kernels for 11%

profile of v4, /device:TPU:1, one launch (start us, length us, event | category | flops | bytes accessed | tf_op | source)
XLA Modules:
  0.0 126.9 jit_solution(2068543270430179234)
XLA Ops:
  6.5 2.2 %start.1 = bf16[128,128]{1,0:T(8,128)(2,1)} custom-call(bf16[1,4,2,128,128]{4,3,2,1,0:T(8,128)(2,1)} %refs_6_.2, bf16[64,128]{1,0:T(8,128)(2,1)} %constant.18.clone.refs_1_.refs_6_, bf16[64,256]{1,0:T(8,128)(2,1)} %constant.19.clone.refs_2_), custom_call_target="tpu_custom_call" | custom-call | tf_op jit(solution)/shard_map/start/pallas_call | solution.py:468
  8.8 11.6 %all-to-all-start = ((bf16[64,2,128]{2,1,0:T(2,128)(2,1)}), bf16[64,2,128]{2,1,0:T(2,128)(2,1)S(1)}, u32[]{:S(2)}, u32[]{:S(2)}) async-start(bf16[64,2,128]{2,1,0:T(2,128)(2,1)} %bitcast.1), calls=%async_computation | async-start | bytes 65536 | tf_op jit(solution)/shard_map/all_to_all | solution.py:482
  20.4 0.0 all-gather.3.cloned.1.call-start
  20.5 1.7 %reshape.21.refs_2_ = bf16[2,2,128,256]{3,2,1,0:T(8,128)(2,1)} reshape(bf16[2,2,32,4,256]{4,3,2,1,0:T(4,128)(2,1)} %param.16) | data formatting | bytes 524288 | tf_op jit(solution)/shard_map/reshape | solution.py:510
  22.2 3.0 %fold.1 = (bf16[8,64,256]{2,1,0:T(8,128)(2,1)}, bf16[2,128,256]{2,1,0:T(8,128)(2,1)}) custom-call(bf16[4,32]{1,0:T(4,128)(2,1)} %refs_3_.1, bf16[1,32]{1,0:T(2,128)(2,1)} %bitcast.19, bf16[2,2,128,256]{3,2,1,0:T(8,128)(2,1)} %reshape.21.refs_2_), custom_call_target="tpu_custom_call" | custom-call | tf_op jit(solution)/shard_map/fold/pallas_call | solution.py:468
  25.2 4.5 %all-to-all-done = bf16[64,2,128]{2,1,0:T(2,128)(2,1)S(1)} async-done(((bf16[64,2,128]{2,1,0:T(2,128)(2,1)}), bf16[64,2,128]{2,1,0:T(2,128)(2,1)S(1)}, u32[]{:S(2)}, u32[]{:S(2)}) %all-to-all-start) | async-done | bytes 32800 | tf_op jit(solution)/shard_map/all_to_all | solution.py:482
  29.7 0.0 all-gather.3.cloned.1.call-update
  29.7 10.1 %all-to-all-start.1 = ((bf16[8,64,256]{2,1,0:T(8,128)(2,1)}), bf16[8,64,256]{2,1,0:T(8,128)(2,1)S(1)}, u32[]{:S(2)}, u32[]{:S(2)}) async-start(bf16[8,64,256]{2,1,0:T(8,128)(2,1)} %get-tuple-element.26), calls=%async_computation.1 | async-start | bytes 524288 | tf_op jit(solution)/shard_map/all_to_all | solution.py:482
  39.8 2.8 %spread.1 = (bf16[512,512]{1,0:T(8,128)(2,1)S(1)}, bf16[512,128]{1,0:T(8,128)(2,1)S(1)}, f32[2,512,128]{2,1,0:T(8,128)S(1)}, bf16[512,256]{1,0:T(8,128)(2,1)S(1)...) custom-call(s32[1]{0:T(128)} %bitcast.refs_0_, ...), custom_call_target="tpu_custom_call" | custom-call | tf_op jit(solution)/shard_map/spread/pallas_call | solution.py:468
  42.6 7.6 %all-to-all-done.1.refs_2_ = bf16[8,64,256]{2,1,0:T(8,128)(2,1)S(1)} async-done(((bf16[8,64,256]{2,1,0:T(8,128)(2,1)}), bf16[8,64,256]{2,1,0:T(8,128)(2,1)S(1)}, u32[]{:S(2)}, u32[]{:S(2)}) %all-to-all-start.1) | async-done | bytes 262176 | tf_op jit(solution)/shard_map/all_to_all | solution.py:482
  50.2 0.9 mix0.1
  51.2 19.7 %all_to_all.50 = bf16[64,16,128]{2,1,0:T(8,128)(2,1)S(1)} all-to-all(bf16[64,16,128]{2,1,0:T(8,128)(2,1)S(1)} %bitcast.15), channel_id=1, replica_groups=mesh['section'=8,'slab'=64] {'slab'}, dimensions={0} | all-to-all | bytes 524288 | tf_op jit(solution)/shard_map/all_to_all | solution.py:482
  70.8 6.5 %middle.1 = (bf16[32,2,128,128]{3,2,1,0:T(8,128)(2,1)}, bf16[1024,128]{1,0:T(8,128)(2,1)S(1)}) custom-call(bf16[1024,128]{1,0:T(8,128)(2,1)S(1)} %bitcast.13, bf16[512,128]{1,0:T(8,128)(2,1)S(1)} %get-tuple-element.30.refs_1_, f32[2,512,128]{2,1,0:T(8,128)S(1)} %get-tuple-element.31.refs_2_, bf16[256,512]{1,0:T(8,128)(2,1)S(1)} %get-tuple-element.32.refs_3_, ...), custom_call_target="tpu_custom_call" | custom-call | tf_op jit(solution)/shard_map/middle/pallas_call | solution.py:468
  77.4 17.8 %all_to_all.51 = bf16[64,16,128]{2,1,0:T(8,128)(2,1)S(1)} all-to-all(bf16[64,16,128]{2,1,0:T(8,128)(2,1)S(1)} %bitcast.16), channel_id=1, replica_groups=mesh['section'=8,'slab'=64] {'slab'}, dimensions={0} | all-to-all | bytes 524288 | tf_op jit(solution)/shard_map/all_to_all | solution.py:482
  95.2 0.0 all-gather.3.cloned.1.call-done
  95.2 1.7 %mix1.1 = bf16[1024,128]{1,0:T(8,128)(2,1)S(1)} custom-call(s32[1]{0:T(128)} %bitcast.refs_0_, bf16[1024,128]{1,0:T(8,128)(2,1)S(1)} %bitcast.11, bf16[2112,128]{1,0:T(8,128)(2,1)S(1)} %get-tuple-element.29.refs_4_.refs_2_, bf16[8,2,128,256]{3,2,1,0:T(8,128)(2,1)} %bitcast.18), custom_call_target="tpu_custom_call" | custom-call | tf_op jit(solution)/shard_map/mix1/pallas_call | solution.py:468
  97.0 17.8 %all_to_all.52 = bf16[64,16,128]{2,1,0:T(8,128)(2,1)S(1)} all-to-all(bf16[64,16,128]{2,1,0:T(8,128)(2,1)S(1)} %bitcast.14), channel_id=1, replica_groups=mesh['section'=8,'slab'=64] {'slab'}, dimensions={0} | all-to-all | bytes 524288 | tf_op jit(solution)/shard_map/all_to_all | solution.py:482
  114.8 5.3 %last.1 = bf16[1,32,2,128,128]{4,3,2,1,0:T(8,128)(2,1)} custom-call(bf16[1024,128]{1,0:T(8,128)(2,1)S(1)} %bitcast.12, bf16[512,512]{1,0:T(8,128)(2,1)S(1)} %get-tuple-element.37.refs_1_, f32[2,512,128]{2,1,0:T(8,128)S(1)} %get-tuple-element.31.refs_2_, bf16[256,512]{1,0:T(8,128)(2,1)S(1)} %get-tuple-element.32.refs_3_, ...), custom_call_target="tpu_custom_call" | custom-call | tf_op jit(solution)/shard_map/last/pallas_call | solution.py:468
Async XLA Ops:
  8.8 20.9 %all-to-all-start = ((bf16[64,2,128]{2,1,0:T(2,128)(2,1)}), bf16[64,2,128]{2,1,0:T(2,128)(2,1)S(1)}, u32[]{:S(2)}, u32[]{:S(2)}) async-start(bf16[64,2,128]{2,1,0:T(2,128)(2,1)} %bitcast.1), calls=%async_computation | async-start | bytes 65536 | tf_op jit(solution)/shard_map/all_to_all | solution.py:482
  20.4 74.8 %all-gather.3.cloned.1.call-start = ((), (), s32[]{:S(2)}) async-start(), calls=%async_computation.5 | async-start | bytes 1179648 | tf_op jit(solution)/shard_map/all_gather | solution.py:520
  29.7 20.5 %all-to-all-start.1 = ((bf16[8,64,256]{2,1,0:T(8,128)(2,1)}), bf16[8,64,256]{2,1,0:T(8,128)(2,1)S(1)}, u32[]{:S(2)}, u32[]{:S(2)}) async-start(bf16[8,64,256]{2,1,0:T(8,128)(2,1)} %get-tuple-element.26), calls=%async_computation.1 | async-start | bytes 524288 | tf_op jit(solution)/shard_map/all_to_all | solution.py:482
Sparse Core Ops, SparseCore 0:
  29.9 38.7 all-gather.2

commit v5 on v4

--- a/solution.py
+++ b/solution.py
@@ -88,8 +88,8 @@
 
 def spread_kernel(
     place_ref, one_x_ref, bypass_ref, lift_ref, bypass_bias_ref, lift_bias_ref, pair_y_ref,
-    one_y_ref, one_z_ref, z_ref, x_ref, kb_ref, kc_ref, bias_ref, fwd_y_ref, inv_y_ref, ones_ref,
-    z_out, x_out,
+    one_y_ref, one_z_ref, z_ref, x_ref, kb_hbm, kc_ref, bias0_ref, bias1_hbm, fwd_y_hbm,
+    inv_y_ref, ones_ref, z_out, x_out, kb_ref, bias1_ref, fwd_y_ref, sem,
 ):
     z_out[...] = z_ref[...]
     x_out[...] = x_ref[...]
@@ -98,6 +98,7 @@
     row, col = picks(512, 512)
     tall = nt_dot(expand, bypass_ref[1]).astype(BF)
     kb_ref[...] = jnp.where((row % 16) == (col % 16), nt_dot(tall, expand), 0.0).astype(BF)
+    kept = fetch([(kb_ref, kb_hbm, sem.at[0])])
     joint = dot(lift_ref[...], bypass_ref[0])
     high = joint.astype(BF)
     low = (joint - high.astype(F32)).astype(BF)
@@ -119,10 +120,11 @@
         bypass_ref[0], column(lift_bias_ref[...]).astype(BF), (((0,), (0,)), ((), ())),
         preferred_element_type=F32,
     )
-    for index, value in enumerate((shift, column(bypass_bias_ref[1:2]))):
-        bias_ref[index] = jnp.dot(
+    for bias_ref, value in ((bias0_ref, shift), (bias1_ref, column(bypass_bias_ref[1:2]))):
+        bias_ref[...] = jnp.dot(
             expand.astype(F32), value, precision=lax.Precision.HIGHEST, preferred_element_type=F32
         )
+    kept += fetch([(bias1_ref, bias1_hbm, sem.at[1])])
     row, col = picks(256, 64)
     repeat = one_hot((row // 64 == col // 16) & (row % 16 == col % 16))
     tall = dot(repeat, pair_y_ref[...])
@@ -136,6 +138,7 @@
     for c in range(4):
         block = jnp.where((col // 16) % 4 == c, wide, 0.0).astype(BF)
         fwd_y_ref[c * 128 : c * 128 + 128, :] = block
+    kept += fetch([(fwd_y_ref, fwd_y_hbm, sem.at[2])])
     place = place_ref[0]
     xr, xi = one_x_ref[place // 2, 0:1, :], one_x_ref[place // 2, 1:2, :]
     yr = jnp.where(place % 2 == 0, one_y_ref[0, 0:1, :], one_y_ref[1, 0:1, :])
@@ -143,10 +146,12 @@
     pr, pi = xr * yr - xi * yi, xr * yi + xi * yr
     zr, zi = one_z_ref[0], one_z_ref[1]
     ones_ref[...] = jnp.concatenate([zr * pr - zi * pi, zr * pi + zi * pr], axis=0)
-
-
-def fold_kernel(lift_ref, lift_bias_ref, weight_hbm, out_ref, later_hbm, weight, later, sem):
-    copy, passed = fetch([(weight_hbm.at[0], weight, sem.at[0]), (weight_hbm.at[1], later, sem.at[1])])
+    for copy in kept:
+        copy.wait()
+
+
+def fold_kernel(lift_ref, lift_bias_ref, weight_hbm, out_ref, weight, sem):
+    (copy,) = fetch([(weight_hbm.at[0], weight, sem.at[0])])
     row, col = picks(HALF, 4)
     pick = one_hot((row % 8 == col))
     row, col = picks(HALF, HALF)
@@ -154,14 +159,11 @@
     row, col = picks(HALF, LENGTH)
     lift = dot(lift.astype(BF), one_hot(row == col // 4))
     lift = jnp.where(row // 8 == col % 4, lift, 0.0).astype(BF)
-    passed.wait()
-    (kept,) = fetch([(later, later_hbm, sem.at[2])])
     copy.wait()
     for r in range(2):
         folded = dot(lift, weight[r]).astype(BF)
         for section in range(8):
             out_ref[section, r * HALF : r * HALF + HALF, :] = folded
-    kept.wait()
 
 
 def start_kernel(fields_hbm, pair_y_hbm, fwd_x_hbm, out_ref, fields, pair_y, fwd_x, rows, sem):
@@ -312,7 +314,9 @@
 def mix_kernel(
     place_ref, got_ref, z_ref, weight_hbm, out_ref, weight, turned, modes, pattern, sem
 ):
-    copies = fetch([(weight_hbm.at[pl.ds(2 * g, 2)], weight.at[pl.ds(2 * g, 2)], sem.at[g]) for g in range(4)])
+    copies = fetch(
+        [(weight_hbm.at[pl.ds(2 * g, 2), 1], weight.at[pl.ds(2 * g, 2)], sem.at[g]) for g in range(4)]
+    )
     value = None
     for block in range(8):
         span = slice(block * 128, block * 128 + 128)
@@ -366,29 +370,29 @@
     made = []
     for z in range(2):
         part = field[:, z, span, :].reshape(512, LENGTH)
-        value = bypassed[:, z * 128 : z * 128 + 128] + bias + part
+        value = bypassed[:, z * 128 : z * 128 + 128] + bias[...] + part
         made.append(activate(value).astype(BF))
     return made
 
 
 def middle_kernel(
-    got_ref, kc_ref, bias_ref, inv_y_ref, fwd_y_ref, x_ref, fields_hbm, hidden_hbm, out_ref,
-    fields, rows, field, hidden, sem,
+    got_ref, kc_ref, bias_ref, inv_y_ref, fwd_y_hbm, x_ref, fields_hbm, hidden, out_ref, fields,
+    fwd_y_ref, rows, field, sem,
 ):
-    (copy,) = fetch([(fields_hbm.at[0], fields, sem.at[0])])
+    copies = fetch([(fields_hbm.at[0], fields, sem.at[0]), (fwd_y_hbm, fwd_y_ref, sem.at[1])])
     inverse(got_ref, x_ref, inv_y_ref, rows, field)
-    copy.wait()
+    for copy in copies:
+        copy.wait()
     def apply(block, carry):
         span = pl.ds(pl.multiple_of(block * 16, 16), 16)
         raw = [fields[:, z, span, :].reshape(64, LENGTH) for z in range(2)]
         raw = jnp.concatenate(raw, axis=1)
-        made = pointwise(span, jnp.concatenate([raw, raw], axis=0), kc_ref, bias_ref[0], field)
+        made = pointwise(span, jnp.concatenate([raw, raw], axis=0), kc_ref, bias_ref, field)
         for z in range(2):
             hidden[:, z, span, :] = made[z].reshape(32, 16, LENGTH)
         return carry
 
     lax.fori_loop(0, 8, apply, 0, unroll=UNROLL_B)
-    (kept,) = fetch([(hidden, hidden_hbm, sem.at[1])])
     def forward(index, carry):
         g, z = index // 2, index % 2
         stacked = []
@@ -405,26 +409,25 @@
 
     lax.fori_loop(0, 8, forward, 0, unroll=UNROLL_A)
     out_ref[...] = rows[...].astype(BF)
-    kept.wait()
 
 
 def last_kernel(
-    got_ref, kb_ref, bias_ref, inv_y_ref, x_ref, hidden_hbm, out_hbm, hidden, rows, field, made_ref,
-    sem,
+    got_ref, kb_hbm, bias_hbm, inv_y_ref, x_ref, hidden, out_hbm, kb, bias, rows, field, made_ref, sem
 ):
-    (copy,) = fetch([(hidden_hbm, hidden, sem.at[0])])
+    copies = fetch([(kb_hbm, kb, sem.at[8]), (bias_hbm, bias, sem.at[9])])
     inverse(got_ref, x_ref, inv_y_ref, rows, field)
-    copy.wait()
+    for copy in copies:
+        copy.wait()
 
     def keep(block):
         span = pl.ds(pl.multiple_of(block * 16, 16), 16)
         source, target = made_ref.at[:, :, span, :], out_hbm.at[0, :, :, span, :]
-        return pltpu.make_async_copy(source, target, sem.at[1 + block])
+        return pltpu.make_async_copy(source, target, sem.at[block])
 
     def apply(block, carry):
         span = pl.ds(pl.multiple_of(block * 16, 16), 16)
         raw = [hidden[:, z, span, :].reshape(512, LENGTH) for z in range(2)]
-        made = pointwise(span, jnp.concatenate(raw, axis=1), kb_ref, bias_ref[1], field)
+        made = pointwise(span, jnp.concatenate(raw, axis=1), kb, bias, field)
         for z in range(2):
             made_ref[:, z, span, :] = made[z].reshape(32, 16, LENGTH)
         keep(block).start()
@@ -508,32 +511,29 @@
         spectrum, spectral_weight = tie((spectrum, spectral_weight))
         spectrum = exchange(spectrum)
         weight = spectral_weight.reshape(2, 2, LENGTH, 256)
-        folded, later = call(
-            fold_kernel,
-            "fold",
-            "ffh",
-            [("v", (8, 64, 256), BF), ("h", (2, LENGTH, 256), BF)],
-            [((2, 128, 256), BF), ((2, 128, 256), BF)],
-            sems=3,
+        (folded,) = call(
+            fold_kernel, "fold", "ffh", [("v", (8, 64, 256), BF)], [((2, 128, 256), BF)], sems=1
         )(lift_weight, lift_bias, weight)
-        folded, bypass_weight, later, _ = tie((folded, bypass_weight, later, spectrum))
-        gathered = lax.all_gather(later, "section", axis=0)
+        folded, bypass_weight, weight, _ = tie((folded, bypass_weight, weight, spectrum))
+        gathered = lax.all_gather(weight, "section", axis=0)
         folded = exchange(folded.reshape(512, 256), "section").reshape(8, 64, 256)
-        kb, kc, bias, fwd_y, inv_y, ones, z_table, x_table = call(
+        kb, kc, bias0, bias1, fwd_y, inv_y, ones, z_table, x_table = call(
             spread_kernel,
             "spread",
             "s" + "f" * 10,
             [
-                ("v", (512, 512), BF),
+                ("h", (512, 512), BF),
                 ("v", (512, 128), BF),
-                ("v", (2, 512, LENGTH), F32),
-                ("v", (512, 256), BF),
+                ("v", (512, LENGTH), F32),
+                ("h", (512, LENGTH), F32),
+                ("h", (512, 256), BF),
                 ("v", (256, 512), BF),
                 ("v", (HALF, LENGTH), F32),
                 ("v", (2112, 128), BF),
                 ("v", (320, 256), BF),
             ],
-            [],
+            [((512, 512), BF), ((512, LENGTH), F32), ((512, 256), BF)],
+            sems=3,
         )(
             place, ones_x, bypass_weight, lift_weight, bypass_bias, lift_bias, const["pair_y"],
             ones_y, ones_z, const["z"], const["x"],
@@ -548,11 +548,11 @@
         hidden, spectrum = call(
             middle_kernel,
             "middle",
-            "pppppph",
-            [("h", cube, BF), ("v", packed, BF)],
-            [((4, 2, 128, 128), BF), (packed, F32), (cube, F32), (cube, BF)],
+            "pppphph",
+            [("v", cube, BF), ("v", packed, BF)],
+            [((4, 2, 128, 128), BF), ((512, 256), BF), (packed, F32), (cube, F32)],
             sems=2,
-        )(exchange(planes), kc, bias, inv_y, fwd_y, x_table, fields)
+        )(exchange(planes), kc, bias0, inv_y, fwd_y, x_table, fields)
         (planes,) = call(
             mix_kernel,
             "mix1",
@@ -567,11 +567,11 @@
         (features,) = call(
             last_kernel,
             "last",
-            "ppppph",
+            "phhppp",
             [("h", (1,) + cube, BF)],
-            [(cube, BF), (packed, F32), (cube, F32), (cube, BF)],
-            sems=9,
-        )(exchange(planes), kb, bias, inv_y, x_table, hidden)
+            [((512, 512), BF), ((512, LENGTH), F32), (packed, F32), (cube, F32), (cube, BF)],
+            sems=10,
+        )(exchange(planes), kb, bias1, inv_y, x_table, hidden)
         return features
 
     placed = (

time: 127 us -> 127 us (level)
  no operation moved by 1% of the time
where the time goes in v5:
time: 127 us
  blocking collectives  54.9 us (43%)
  Pallas kernels  22.8 us (18%)
  starting transfers between devices  21.7 us (17%)
  between operations  13.5 us (11%)
  waiting for transfers between devices  12.2 us (10%)
  local copies, waits for them, and re-layouts  1.72 us (1%)
    all_to_all x3, blocking collectives, exchange(): return lax.all_to_all(value, axis, split_axis=0, concat_axis=0, tiled=True)  54.9 us
    pallas_call x7, Pallas kernels, run(): pl.pallas_call(body, name=name, out_shape=[spaces[letter](shape, kind) fo...  22.8 us
    all_to_all x2, starting transfers between devices, exchange(): return lax.all_to_all(value, axis, split_axis=0, concat_axis=0, tiled=True)  21.7 us
    all_to_all x2, waiting for transfers between devices, exchange(): return lax.all_to_all(value, axis, split_axis=0, concat_axis=0, tiled=True)  12.2 us
  transfers between devices with their start and end apart: 3, of which 2 were waited for; matrix products, arithmetic and copies ran while one was open for 1% of the time, Pallas kernels for 11%

profile of v5, /device:TPU:1, one launch (start us, length us, event | category | flops | bytes accessed | tf_op | source)
XLA Modules:
  0.0 126.9 jit_solution(2666725499600254769)
XLA Ops:
  6.5 2.2 %start.1 = bf16[128,128]{1,0:T(8,128)(2,1)} custom-call(bf16[1,4,2,128,128]{4,3,2,1,0:T(8,128)(2,1)} %refs_6_.2, bf16[64,128]{1,0:T(8,128)(2,1)} %constant.18.clone.refs_1_.refs_6_, bf16[64,256]{1,0:T(8,128)(2,1)} %constant.19.clone.refs_2_), custom_call_target="tpu_custom_call" | custom-call | tf_op jit(solution)/shard_map/start/pallas_call | solution.py:471
  8.8 11.6 %all-to-all-start = ((bf16[64,2,128]{2,1,0:T(2,128)(2,1)}), bf16[64,2,128]{2,1,0:T(2,128)(2,1)S(1)}, u32[]{:S(2)}, u32[]{:S(2)}) async-start(bf16[64,2,128]{2,1,0:T(2,128)(2,1)} %bitcast.1), calls=%async_computation | async-start | bytes 65536 | tf_op jit(solution)/shard_map/all_to_all | solution.py:485
  20.4 0.0 all-gather.3.cloned.1.call-start
  20.5 1.7 %reshape.21.refs_2_ = bf16[2,2,128,256]{3,2,1,0:T(8,128)(2,1)} reshape(bf16[2,2,32,4,256]{4,3,2,1,0:T(4,128)(2,1)} %param.16) | data formatting | bytes 524288 | tf_op jit(solution)/shard_map/reshape | solution.py:513
  22.2 2.5 %fold.1 = bf16[8,64,256]{2,1,0:T(8,128)(2,1)} custom-call(bf16[4,32]{1,0:T(4,128)(2,1)} %refs_3_.1, bf16[1,32]{1,0:T(2,128)(2,1)} %bitcast.19, bf16[2,2,128,256]{3,2,1,0:T(8,128)(2,1)} %reshape.21.refs_2_), custom_call_target="tpu_custom_call" | custom-call | tf_op jit(solution)/shard_map/fold/pallas_call | solution.py:471
  24.7 5.0 %all-to-all-done = bf16[64,2,128]{2,1,0:T(2,128)(2,1)S(1)} async-done(((bf16[64,2,128]{2,1,0:T(2,128)(2,1)}), bf16[64,2,128]{2,1,0:T(2,128)(2,1)S(1)}, u32[]{:S(2)}, u32[]{:S(2)}) %all-to-all-start) | async-done | bytes 32800 | tf_op jit(solution)/shard_map/all_to_all | solution.py:485
  29.7 0.0 all-gather.3.cloned.1.call-update
  29.7 10.0 %all-to-all-start.1 = ((bf16[8,64,256]{2,1,0:T(8,128)(2,1)}), bf16[8,64,256]{2,1,0:T(8,128)(2,1)S(1)}, u32[]{:S(2)}, u32[]{:S(2)}) async-start(bf16[8,64,256]{2,1,0:T(8,128)(2,1)} %fold.1), calls=%async_computation.1 | async-start | bytes 524288 | tf_op jit(solution)/shard_map/all_to_all | solution.py:485
  39.8 3.6 %spread.1 = (bf16[512,512]{1,0:T(8,128)(2,1)}, bf16[512,128]{1,0:T(8,128)(2,1)S(1)}, f32[512,128]{1,0:T(8,128)S(1)}, f32[512,128]{1,0:T(8,128)}, bf16[512,256]{1...) custom-call(s32[1]{0:T(128)} %bitcast.refs_0_, ...), custom_call_target="tpu_custom_call" | custom-call | tf_op jit(solution)/shard_map/spread/pallas_call | solution.py:471
  43.4 7.2 %all-to-all-done.1.refs_2_ = bf16[8,64,256]{2,1,0:T(8,128)(2,1)S(1)} async-done(((bf16[8,64,256]{2,1,0:T(8,128)(2,1)}), bf16[8,64,256]{2,1,0:T(8,128)(2,1)S(1)}, u32[]{:S(2)}, u32[]{:S(2)}) %all-to-all-start.1) | async-done | bytes 262176 | tf_op jit(solution)/shard_map/all_to_all | solution.py:485
  50.5 0.9 mix0.1
  51.5 19.2 %all_to_all.50 = bf16[64,16,128]{2,1,0:T(8,128)(2,1)S(1)} all-to-all(bf16[64,16,128]{2,1,0:T(8,128)(2,1)S(1)} %bitcast.13), channel_id=1, replica_groups=mesh['section'=8,'slab'=64] {'slab'}, dimensions={0} | all-to-all | bytes 524288 | tf_op jit(solution)/shard_map/all_to_all | solution.py:485
  70.7 6.5 %middle.1 = (bf16[32,2,128,128]{3,2,1,0:T(8,128)(2,1)S(1)}, bf16[1024,128]{1,0:T(8,128)(2,1)S(1)}) custom-call(bf16[1024,128]{1,0:T(8,128)(2,1)S(1)} %bitcast.12, bf16[512,128]{1,0:T(8,128)(2,1)S(1)} %get-tuple-element.27.refs_1_, f32[512,128]{1,0:T(8,128)S(1)} %get-tuple-element.28.refs_2_, bf16[256,512]{1,0:T(8,128)(2,1)S(1)} %get-tuple-element.29.refs_3_, ...), custom_call_target="tpu_custom_call" | custom-call | tf_op jit(solution)/shard_map/middle/pallas_call | solution.py:471
  77.2 17.9 %all_to_all.51 = bf16[64,16,128]{2,1,0:T(8,128)(2,1)S(1)} all-to-all(bf16[64,16,128]{2,1,0:T(8,128)(2,1)S(1)} %bitcast.16), channel_id=1, replica_groups=mesh['section'=8,'slab'=64] {'slab'}, dimensions={0} | all-to-all | bytes 524288 | tf_op jit(solution)/shard_map/all_to_all | solution.py:485
  95.1 0.0 all-gather.3.cloned.1.call-done
  95.1 1.7 %mix1.1 = bf16[1024,128]{1,0:T(8,128)(2,1)S(1)} custom-call(s32[1]{0:T(128)} %bitcast.refs_0_, bf16[1024,128]{1,0:T(8,128)(2,1)S(1)} %bitcast.14, bf16[2112,128]{1,0:T(8,128)(2,1)S(1)} %get-tuple-element.26.refs_4_.refs_2_, bf16[8,2,2,128,256]{4,3,2,1,0:T(8,128)(2,1)} %bitcast.18), custom_call_target="tpu_custom_call" | custom-call | tf_op jit(solution)/shard_map/mix1/pallas_call | solution.py:471
  96.9 17.8 %all_to_all.52 = bf16[64,16,128]{2,1,0:T(8,128)(2,1)S(1)} all-to-all(bf16[64,16,128]{2,1,0:T(8,128)(2,1)S(1)} %bitcast.15), channel_id=1, replica_groups=mesh['section'=8,'slab'=64] {'slab'}, dimensions={0} | all-to-all | bytes 524288 | tf_op jit(solution)/shard_map/all_to_all | solution.py:485
  114.7 5.3 %last.1 = bf16[1,32,2,128,128]{4,3,2,1,0:T(8,128)(2,1)} custom-call(bf16[1024,128]{1,0:T(8,128)(2,1)S(1)} %bitcast.11, bf16[512,512]{1,0:T(8,128)(2,1)} %get-tuple-element.34.refs_1_, f32[512,128]{1,0:T(8,128)} %get-tuple-element.35.refs_2_, bf16[256,512]{1,0:T(8,128)(2,1)S(1)} %get-tuple-element.29.refs_3_, ...), custom_call_target="tpu_custom_call" | custom-call | tf_op jit(solution)/shard_map/last/pallas_call | solution.py:471
Async XLA Ops:
  8.8 20.9 %all-to-all-start = ((bf16[64,2,128]{2,1,0:T(2,128)(2,1)}), bf16[64,2,128]{2,1,0:T(2,128)(2,1)S(1)}, u32[]{:S(2)}, u32[]{:S(2)}) async-start(bf16[64,2,128]{2,1,0:T(2,128)(2,1)} %bitcast.1), calls=%async_computation | async-start | bytes 65536 | tf_op jit(solution)/shard_map/all_to_all | solution.py:485
  20.4 74.7 %all-gather.3.cloned.1.call-start = ((), (), s32[]{:S(2)}) async-start(), calls=%async_computation.5 | async-start | bytes 2359296 | tf_op jit(solution)/shard_map/all_gather | solution.py:518
  29.7 20.8 %all-to-all-start.1 = ((bf16[8,64,256]{2,1,0:T(8,128)(2,1)}), bf16[8,64,256]{2,1,0:T(8,128)(2,1)S(1)}, u32[]{:S(2)}, u32[]{:S(2)}) async-start(bf16[8,64,256]{2,1,0:T(8,128)(2,1)} %fold.1), calls=%async_computation.1 | async-start | bytes 524288 | tf_op jit(solution)/shard_map/all_to_all | solution.py:485
Sparse Core Ops, SparseCore 0:
  29.9 42.0 all-gather.2

commit v6 on v5

--- a/solution.py
+++ b/solution.py
@@ -14,6 +14,7 @@
 LENGTH = 128
 SLABS = 64
 UNROLL_A = 4
+UNROLL_F = 8
 UNROLL_B = 8
 BF = jnp.bfloat16
 F32 = jnp.float32
@@ -150,8 +151,16 @@
         copy.wait()
 
 
-def fold_kernel(lift_ref, lift_bias_ref, weight_hbm, out_ref, weight, sem):
-    (copy,) = fetch([(weight_hbm.at[0], weight, sem.at[0])])
+def fold_kernel(lift_hbm, lift_bias_hbm, weight_hbm, out_ref, lift_ref, lift_bias_ref, weight, sem):
+    copy, *small = fetch(
+        [
+            (weight_hbm.at[0], weight, sem.at[0]),
+            (lift_hbm, lift_ref, sem.at[1]),
+            (lift_bias_hbm, lift_bias_ref, sem.at[2]),
+        ]
+    )
+    for part in small:
+        part.wait()
     row, col = picks(HALF, 4)
     pick = one_hot((row % 8 == col))
     row, col = picks(HALF, HALF)
@@ -407,7 +416,7 @@
                 rows[pl.ds(at, 32, stride=32), :] = value[r * 32 : r * 32 + 32]
         return carry
 
-    lax.fori_loop(0, 8, forward, 0, unroll=UNROLL_A)
+    lax.fori_loop(0, 8, forward, 0, unroll=UNROLL_F)
     out_ref[...] = rows[...].astype(BF)
 
 
@@ -512,7 +521,12 @@
         spectrum = exchange(spectrum)
         weight = spectral_weight.reshape(2, 2, LENGTH, 256)
         (folded,) = call(
-            fold_kernel, "fold", "ffh", [("v", (8, 64, 256), BF)], [((2, 128, 256), BF)], sems=1
+            fold_kernel,
+            "fold",
+            "hhh",
+            [("v", (8, 64, 256), BF)],
+            [((4, 32), BF), ((1, 32), BF), ((2, 128, 256), BF)],
+            sems=3,
         )(lift_weight, lift_bias, weight)
         folded, bypass_weight, weight, _ = tie((folded, bypass_weight, weight, spectrum))
         gathered = lax.all_gather(weight, "section", axis=0)

time: 127 us -> 127 us (level)
  waiting for transfers between devices: 12.2 us -> 13.5 us
    all_to_all x2, waiting for transfers between devices: 12.2 us -> 13.5 us  [exchange(): return lax.all_to_all(value, axis, split_axis=0, concat_axis=0, tiled=True)]
  transfers between devices with their start and end apart: 3 -> 3, of which waited for: 2 -> 2; matrix products, arithmetic and copies ran while one was open for 1% -> 1% of each run, Pallas kernels for 11% -> 10%
where the time goes in v6:
time: 127 us
  blocking collectives  54.7 us (43%)
  Pallas kernels  21.8 us (17%)
  starting transfers between devices  21.7 us (17%)
  waiting for transfers between devices  13.5 us (11%)
  between operations  13.5 us (11%)
  local copies, waits for them, and re-layouts  1.72 us (1%)
    all_to_all x3, blocking collectives, exchange(): return lax.all_to_all(value, axis, split_axis=0, concat_axis=0, tiled=True)  54.7 us
    pallas_call x7, Pallas kernels, run(): pl.pallas_call(body, name=name, out_shape=[spaces[letter](shape, kind) fo...  21.8 us
    all_to_all x2, starting transfers between devices, exchange(): return lax.all_to_all(value, axis, split_axis=0, concat_axis=0, tiled=True)  21.7 us
    all_to_all x2, waiting for transfers between devices, exchange(): return lax.all_to_all(value, axis, split_axis=0, concat_axis=0, tiled=True)  13.5 us
  transfers between devices with their start and end apart: 3, of which 2 were waited for; matrix products, arithmetic and copies ran while one was open for 1% of the time, Pallas kernels for 10%

profile of v6, /device:TPU:1, one launch (start us, length us, event | category | flops | bytes accessed | tf_op | source)
XLA Modules:
  0.0 127.0 jit_solution(4651954089094040741)
XLA Ops:
  6.5 2.2 %start.1 = bf16[128,128]{1,0:T(8,128)(2,1)} custom-call(bf16[1,4,2,128,128]{4,3,2,1,0:T(8,128)(2,1)} %refs_6_.2, bf16[64,128]{1,0:T(8,128)(2,1)} %constant.18.clone.refs_1_.refs_6_, bf16[64,256]{1,0:T(8,128)(2,1)} %constant.19.clone.refs_2_), custom_call_target="tpu_custom_call" | custom-call | tf_op jit(solution)/shard_map/start/pallas_call | solution.py:480
  8.8 11.6 %all-to-all-start = ((bf16[64,2,128]{2,1,0:T(2,128)(2,1)}), bf16[64,2,128]{2,1,0:T(2,128)(2,1)S(1)}, u32[]{:S(2)}, u32[]{:S(2)}) async-start(bf16[64,2,128]{2,1,0:T(2,128)(2,1)} %bitcast.1), calls=%async_computation | async-start | bytes 65536 | tf_op jit(solution)/shard_map/all_to_all | solution.py:494
  20.4 0.0 all-gather.3.cloned.1.call-start
  20.5 1.7 %reshape.21.refs_2_ = bf16[2,2,128,256]{3,2,1,0:T(8,128)(2,1)} reshape(bf16[2,2,32,4,256]{4,3,2,1,0:T(4,128)(2,1)} %param.16) | data formatting | bytes 524288 | tf_op jit(solution)/shard_map/reshape | solution.py:522
  22.2 1.9 %fold.1 = bf16[8,64,256]{2,1,0:T(8,128)(2,1)} custom-call(bf16[4,32]{1,0:T(4,128)(2,1)} %refs_3_.1, bf16[1,32]{1,0:T(2,128)(2,1)} %bitcast.19, bf16[2,2,128,256]{3,2,1,0:T(8,128)(2,1)} %reshape.21.refs_2_), custom_call_target="tpu_custom_call" | custom-call | tf_op jit(solution)/shard_map/fold/pallas_call | solution.py:480
  24.1 5.6 %all-to-all-done = bf16[64,2,128]{2,1,0:T(2,128)(2,1)S(1)} async-done(((bf16[64,2,128]{2,1,0:T(2,128)(2,1)}), bf16[64,2,128]{2,1,0:T(2,128)(2,1)S(1)}, u32[]{:S(2)}, u32[]{:S(2)}) %all-to-all-start) | async-done | bytes 32800 | tf_op jit(solution)/shard_map/all_to_all | solution.py:494
  29.7 0.0 all-gather.3.cloned.1.call-update
  29.7 10.0 %all-to-all-start.1 = ((bf16[8,64,256]{2,1,0:T(8,128)(2,1)}), bf16[8,64,256]{2,1,0:T(8,128)(2,1)S(1)}, u32[]{:S(2)}, u32[]{:S(2)}) async-start(bf16[8,64,256]{2,1,0:T(8,128)(2,1)} %fold.1), calls=%async_computation.1 | async-start | bytes 524288 | tf_op jit(solution)/shard_map/all_to_all | solution.py:494
  39.8 3.6 %spread.1 = (bf16[512,512]{1,0:T(8,128)(2,1)}, bf16[512,128]{1,0:T(8,128)(2,1)S(1)}, f32[512,128]{1,0:T(8,128)S(1)}, f32[512,128]{1,0:T(8,128)}, bf16[512,256]{1...) custom-call(s32[1]{0:T(128)} %bitcast.refs_0_, ...), custom_call_target="tpu_custom_call" | custom-call | tf_op jit(solution)/shard_map/spread/pallas_call | solution.py:480
  43.4 7.9 %all-to-all-done.1.refs_2_ = bf16[8,64,256]{2,1,0:T(8,128)(2,1)S(1)} async-done(((bf16[8,64,256]{2,1,0:T(8,128)(2,1)}), bf16[8,64,256]{2,1,0:T(8,128)(2,1)S(1)}, u32[]{:S(2)}, u32[]{:S(2)}) %all-to-all-start.1) | async-done | bytes 262176 | tf_op jit(solution)/shard_map/all_to_all | solution.py:494
  51.2 0.9 mix0.1
  52.2 19.0 %all_to_all.50 = bf16[64,16,128]{2,1,0:T(8,128)(2,1)S(1)} all-to-all(bf16[64,16,128]{2,1,0:T(8,128)(2,1)S(1)} %bitcast.13), channel_id=1, replica_groups=mesh['section'=8,'slab'=64] {'slab'}, dimensions={0} | all-to-all | bytes 524288 | tf_op jit(solution)/shard_map/all_to_all | solution.py:494
  71.2 6.2 %middle.1 = (bf16[32,2,128,128]{3,2,1,0:T(8,128)(2,1)S(1)}, bf16[1024,128]{1,0:T(8,128)(2,1)S(1)}) custom-call(bf16[1024,128]{1,0:T(8,128)(2,1)S(1)} %bitcast.12, bf16[512,128]{1,0:T(8,128)(2,1)S(1)} %get-tuple-element.27.refs_1_, f32[512,128]{1,0:T(8,128)S(1)} %get-tuple-element.28.refs_2_, bf16[256,512]{1,0:T(8,128)(2,1)S(1)} %get-tuple-element.29.refs_3_, ...), custom_call_target="tpu_custom_call" | custom-call | tf_op jit(solution)/shard_map/middle/pallas_call | solution.py:480
  77.4 17.9 %all_to_all.51 = bf16[64,16,128]{2,1,0:T(8,128)(2,1)S(1)} all-to-all(bf16[64,16,128]{2,1,0:T(8,128)(2,1)S(1)} %bitcast.16), channel_id=1, replica_groups=mesh['section'=8,'slab'=64] {'slab'}, dimensions={0} | all-to-all | bytes 524288 | tf_op jit(solution)/shard_map/all_to_all | solution.py:494
  95.3 0.0 all-gather.3.cloned.1.call-done
  95.3 1.7 %mix1.1 = bf16[1024,128]{1,0:T(8,128)(2,1)S(1)} custom-call(s32[1]{0:T(128)} %bitcast.refs_0_, bf16[1024,128]{1,0:T(8,128)(2,1)S(1)} %bitcast.14, bf16[2112,128]{1,0:T(8,128)(2,1)S(1)} %get-tuple-element.26.refs_4_.refs_2_, bf16[8,2,2,128,256]{4,3,2,1,0:T(8,128)(2,1)} %bitcast.18), custom_call_target="tpu_custom_call" | custom-call | tf_op jit(solution)/shard_map/mix1/pallas_call | solution.py:480
  97.0 17.8 %all_to_all.52 = bf16[64,16,128]{2,1,0:T(8,128)(2,1)S(1)} all-to-all(bf16[64,16,128]{2,1,0:T(8,128)(2,1)S(1)} %bitcast.15), channel_id=1, replica_groups=mesh['section'=8,'slab'=64] {'slab'}, dimensions={0} | all-to-all | bytes 524288 | tf_op jit(solution)/shard_map/all_to_all | solution.py:494
  114.9 5.3 %last.1 = bf16[1,32,2,128,128]{4,3,2,1,0:T(8,128)(2,1)} custom-call(bf16[1024,128]{1,0:T(8,128)(2,1)S(1)} %bitcast.11, bf16[512,512]{1,0:T(8,128)(2,1)} %get-tuple-element.34.refs_1_, f32[512,128]{1,0:T(8,128)} %get-tuple-element.35.refs_2_, bf16[256,512]{1,0:T(8,128)(2,1)S(1)} %get-tuple-element.29.refs_3_, ...), custom_call_target="tpu_custom_call" | custom-call | tf_op jit(solution)/shard_map/last/pallas_call | solution.py:480
Async XLA Ops:
  8.8 20.9 %all-to-all-start = ((bf16[64,2,128]{2,1,0:T(2,128)(2,1)}), bf16[64,2,128]{2,1,0:T(2,128)(2,1)S(1)}, u32[]{:S(2)}, u32[]{:S(2)}) async-start(bf16[64,2,128]{2,1,0:T(2,128)(2,1)} %bitcast.1), calls=%async_computation | async-start | bytes 65536 | tf_op jit(solution)/shard_map/all_to_all | solution.py:494
  20.4 74.8 %all-gather.3.cloned.1.call-start = ((), (), s32[]{:S(2)}) async-start(), calls=%async_computation.5 | async-start | bytes 2359296 | tf_op jit(solution)/shard_map/all_gather | solution.py:532
  29.7 21.5 %all-to-all-start.1 = ((bf16[8,64,256]{2,1,0:T(8,128)(2,1)}), bf16[8,64,256]{2,1,0:T(8,128)(2,1)S(1)}, u32[]{:S(2)}, u32[]{:S(2)}) async-start(bf16[8,64,256]{2,1,0:T(8,128)(2,1)} %fold.1), calls=%async_computation.1 | async-start | bytes 524288 | tf_op jit(solution)/shard_map/all_to_all | solution.py:494
Sparse Core Ops, SparseCore 0:
  29.9 41.9 all-gather.2

commit v7 on v6

--- a/solution.py
+++ b/solution.py
@@ -151,14 +151,19 @@
         copy.wait()
 
 
-def fold_kernel(lift_hbm, lift_bias_hbm, weight_hbm, out_ref, lift_ref, lift_bias_ref, weight, sem):
-    copy, *small = fetch(
+def fold_kernel(
+    lift_hbm, lift_bias_hbm, weight_hbm, out_ref, later_hbm, lift_ref, lift_bias_ref, weight, later, sem
+):
+    passed, copy, *small = fetch(
         [
+            (weight_hbm.at[1], later, sem.at[3]),
             (weight_hbm.at[0], weight, sem.at[0]),
             (lift_hbm, lift_ref, sem.at[1]),
             (lift_bias_hbm, lift_bias_ref, sem.at[2]),
         ]
     )
+    passed.wait()
+    (kept,) = fetch([(later, later_hbm, sem.at[4])])
     for part in small:
         part.wait()
     row, col = picks(HALF, 4)
@@ -173,6 +178,7 @@
         folded = dot(lift, weight[r]).astype(BF)
         for section in range(8):
             out_ref[section, r * HALF : r * HALF + HALF, :] = folded
+    kept.wait()
 
 
 def start_kernel(fields_hbm, pair_y_hbm, fwd_x_hbm, out_ref, fields, pair_y, fwd_x, rows, sem):
@@ -324,7 +330,7 @@
     place_ref, got_ref, z_ref, weight_hbm, out_ref, weight, turned, modes, pattern, sem
 ):
     copies = fetch(
-        [(weight_hbm.at[pl.ds(2 * g, 2), 1], weight.at[pl.ds(2 * g, 2)], sem.at[g]) for g in range(4)]
+        [(weight_hbm.at[pl.ds(2 * g, 2)], weight.at[pl.ds(2 * g, 2)], sem.at[g]) for g in range(4)]
     )
     value = None
     for block in range(8):
@@ -520,16 +526,16 @@
         spectrum, spectral_weight = tie((spectrum, spectral_weight))
         spectrum = exchange(spectrum)
         weight = spectral_weight.reshape(2, 2, LENGTH, 256)
-        (folded,) = call(
+        folded, later = call(
             fold_kernel,
             "fold",
             "hhh",
-            [("v", (8, 64, 256), BF)],
-            [((4, 32), BF), ((1, 32), BF), ((2, 128, 256), BF)],
-            sems=3,
+            [("v", (8, 64, 256), BF), ("h", (2, LENGTH, 256), BF)],
+            [((4, 32), BF), ((1, 32), BF), ((2, 128, 256), BF), ((2, 128, 256), BF)],
+            sems=5,
         )(lift_weight, lift_bias, weight)
-        folded, bypass_weight, weight, _ = tie((folded, bypass_weight, weight, spectrum))
-        gathered = lax.all_gather(weight, "section", axis=0)
+        folded, bypass_weight, later, _ = tie((folded, bypass_weight, later, spectrum))
+        gathered = lax.all_gather(later, "section", axis=0)
         folded = exchange(folded.reshape(512, 256), "section").reshape(8, 64, 256)
         kb, kc, bias0, bias1, fwd_y, inv_y, ones, z_table, x_table = call(
             spread_kernel,

time: 127 us -> 127 us (level)
  no operation moved by 1% of the time
where the time goes in v7:
time: 127 us
  blocking collectives  54.7 us (43%)
  Pallas kernels  22.2 us (17%)
  starting transfers between devices  21.7 us (17%)
  between operations  13.5 us (11%)
  waiting for transfers between devices  12.8 us (10%)
  local copies, waits for them, and re-layouts  1.72 us (1%)
    all_to_all x3, blocking collectives, exchange(): return lax.all_to_all(value, axis, split_axis=0, concat_axis=0, tiled=True)  54.7 us
    pallas_call x7, Pallas kernels, run(): pl.pallas_call(body, name=name, out_shape=[spaces[letter](shape, kind) fo...  22.2 us
    all_to_all x2, starting transfers between devices, exchange(): return lax.all_to_all(value, axis, split_axis=0, concat_axis=0, tiled=True)  21.7 us
    all_to_all x2, waiting for transfers between devices, exchange(): return lax.all_to_all(value, axis, split_axis=0, concat_axis=0, tiled=True)  12.8 us
  transfers between devices with their start and end apart: 3, of which 2 were waited for; matrix products, arithmetic and copies ran while one was open for 1% of the time, Pallas kernels for 10%

profile of v7, /device:TPU:1, one launch (start us, length us, event | category | flops | bytes accessed | tf_op | source)
XLA Modules:
  0.0 126.7 jit_solution(12187875202037754214)
XLA Ops:
  6.5 2.2 %start.1 = bf16[128,128]{1,0:T(8,128)(2,1)} custom-call(bf16[1,4,2,128,128]{4,3,2,1,0:T(8,128)(2,1)} %refs_6_.2, bf16[64,128]{1,0:T(8,128)(2,1)} %constant.18.clone.refs_1_.refs_6_, bf16[64,256]{1,0:T(8,128)(2,1)} %constant.19.clone.refs_2_), custom_call_target="tpu_custom_call" | custom-call | tf_op jit(solution)/shard_map/start/pallas_call | solution.py:486
  8.8 11.6 %all-to-all-start = ((bf16[64,2,128]{2,1,0:T(2,128)(2,1)}), bf16[64,2,128]{2,1,0:T(2,128)(2,1)S(1)}, u32[]{:S(2)}, u32[]{:S(2)}) async-start(bf16[64,2,128]{2,1,0:T(2,128)(2,1)} %bitcast.1), calls=%async_computation | async-start | bytes 65536 | tf_op jit(solution)/shard_map/all_to_all | solution.py:500
  20.4 0.0 all-gather.3.cloned.1.call-start
  20.5 1.7 %reshape.21.refs_2_ = bf16[2,2,128,256]{3,2,1,0:T(8,128)(2,1)} reshape(bf16[2,2,32,4,256]{4,3,2,1,0:T(4,128)(2,1)} %param.16) | data formatting | bytes 524288 | tf_op jit(solution)/shard_map/reshape | solution.py:528
  22.2 2.3 %fold.1 = (bf16[8,64,256]{2,1,0:T(8,128)(2,1)}, bf16[2,128,256]{2,1,0:T(8,128)(2,1)}) custom-call(bf16[4,32]{1,0:T(4,128)(2,1)} %refs_3_.1, bf16[1,32]{1,0:T(2,128)(2,1)} %bitcast.19, bf16[2,2,128,256]{3,2,1,0:T(8,128)(2,1)} %reshape.21.refs_2_), custom_call_target="tpu_custom_call" | custom-call | tf_op jit(solution)/shard_map/fold/pallas_call | solution.py:486
  24.5 5.2 %all-to-all-done = bf16[64,2,128]{2,1,0:T(2,128)(2,1)S(1)} async-done(((bf16[64,2,128]{2,1,0:T(2,128)(2,1)}), bf16[64,2,128]{2,1,0:T(2,128)(2,1)S(1)}, u32[]{:S(2)}, u32[]{:S(2)}) %all-to-all-start) | async-done | bytes 32800 | tf_op jit(solution)/shard_map/all_to_all | solution.py:500
  29.7 0.0 all-gather.3.cloned.1.call-update
  29.7 10.1 %all-to-all-start.1 = ((bf16[8,64,256]{2,1,0:T(8,128)(2,1)}), bf16[8,64,256]{2,1,0:T(8,128)(2,1)S(1)}, u32[]{:S(2)}, u32[]{:S(2)}) async-start(bf16[8,64,256]{2,1,0:T(8,128)(2,1)} %get-tuple-element.27), calls=%async_computation.1 | async-start | bytes 524288 | tf_op jit(solution)/shard_map/all_to_all | solution.py:500
  39.8 3.6 %spread.1 = (bf16[512,512]{1,0:T(8,128)(2,1)}, bf16[512,128]{1,0:T(8,128)(2,1)S(1)}, f32[512,128]{1,0:T(8,128)S(1)}, f32[512,128]{1,0:T(8,128)}, bf16[512,256]{1...) custom-call(s32[1]{0:T(128)} %bitcast.refs_0_, ...), custom_call_target="tpu_custom_call" | custom-call | tf_op jit(solution)/shard_map/spread/pallas_call | solution.py:486
  43.4 7.6 %all-to-all-done.1.refs_2_ = bf16[8,64,256]{2,1,0:T(8,128)(2,1)S(1)} async-done(((bf16[8,64,256]{2,1,0:T(8,128)(2,1)}), bf16[8,64,256]{2,1,0:T(8,128)(2,1)S(1)}, u32[]{:S(2)}, u32[]{:S(2)}) %all-to-all-start.1) | async-done | bytes 262176 | tf_op jit(solution)/shard_map/all_to_all | solution.py:500
  50.9 0.9 mix0.1
  51.9 19.0 %all_to_all.50 = bf16[64,16,128]{2,1,0:T(8,128)(2,1)S(1)} all-to-all(bf16[64,16,128]{2,1,0:T(8,128)(2,1)S(1)} %bitcast.15), channel_id=1, replica_groups=mesh['section'=8,'slab'=64] {'slab'}, dimensions={0} | all-to-all | bytes 524288 | tf_op jit(solution)/shard_map/all_to_all | solution.py:500
  70.8 6.2 %middle.1 = (bf16[32,2,128,128]{3,2,1,0:T(8,128)(2,1)S(1)}, bf16[1024,128]{1,0:T(8,128)(2,1)S(1)}) custom-call(bf16[1024,128]{1,0:T(8,128)(2,1)S(1)} %bitcast.13, bf16[512,128]{1,0:T(8,128)(2,1)S(1)} %get-tuple-element.31.refs_1_, f32[512,128]{1,0:T(8,128)S(1)} %get-tuple-element.32.refs_2_, bf16[256,512]{1,0:T(8,128)(2,1)S(1)} %get-tuple-element.33.refs_3_, ...), custom_call_target="tpu_custom_call" | custom-call | tf_op jit(solution)/shard_map/middle/pallas_call | solution.py:486
  77.0 17.9 %all_to_all.51 = bf16[64,16,128]{2,1,0:T(8,128)(2,1)S(1)} all-to-all(bf16[64,16,128]{2,1,0:T(8,128)(2,1)S(1)} %bitcast.16), channel_id=1, replica_groups=mesh['section'=8,'slab'=64] {'slab'}, dimensions={0} | all-to-all | bytes 524288 | tf_op jit(solution)/shard_map/all_to_all | solution.py:500
  94.9 0.0 all-gather.3.cloned.1.call-done
  94.9 1.7 %mix1.1 = bf16[1024,128]{1,0:T(8,128)(2,1)S(1)} custom-call(s32[1]{0:T(128)} %bitcast.refs_0_, bf16[1024,128]{1,0:T(8,128)(2,1)S(1)} %bitcast.11, bf16[2112,128]{1,0:T(8,128)(2,1)S(1)} %get-tuple-element.30.refs_4_.refs_2_, bf16[8,2,128,256]{3,2,1,0:T(8,128)(2,1)} %bitcast.18), custom_call_target="tpu_custom_call" | custom-call | tf_op jit(solution)/shard_map/mix1/pallas_call | solution.py:486
  96.7 17.8 %all_to_all.52 = bf16[64,16,128]{2,1,0:T(8,128)(2,1)S(1)} all-to-all(bf16[64,16,128]{2,1,0:T(8,128)(2,1)S(1)} %bitcast.14), channel_id=1, replica_groups=mesh['section'=8,'slab'=64] {'slab'}, dimensions={0} | all-to-all | bytes 524288 | tf_op jit(solution)/shard_map/all_to_all | solution.py:500
  114.5 5.3 %last.1 = bf16[1,32,2,128,128]{4,3,2,1,0:T(8,128)(2,1)} custom-call(bf16[1024,128]{1,0:T(8,128)(2,1)S(1)} %bitcast.12, bf16[512,512]{1,0:T(8,128)(2,1)} %get-tuple-element.38.refs_1_, f32[512,128]{1,0:T(8,128)} %get-tuple-element.39.refs_2_, bf16[256,512]{1,0:T(8,128)(2,1)S(1)} %get-tuple-element.33.refs_3_, ...), custom_call_target="tpu_custom_call" | custom-call | tf_op jit(solution)/shard_map/last/pallas_call | solution.py:486
Async XLA Ops:
  8.8 20.9 %all-to-all-start = ((bf16[64,2,128]{2,1,0:T(2,128)(2,1)}), bf16[64,2,128]{2,1,0:T(2,128)(2,1)S(1)}, u32[]{:S(2)}, u32[]{:S(2)}) async-start(bf16[64,2,128]{2,1,0:T(2,128)(2,1)} %bitcast.1), calls=%async_computation | async-start | bytes 65536 | tf_op jit(solution)/shard_map/all_to_all | solution.py:500
  20.4 74.5 %all-gather.3.cloned.1.call-start = ((), (), s32[]{:S(2)}) async-start(), calls=%async_computation.5 | async-start | bytes 1179648 | tf_op jit(solution)/shard_map/all_gather | solution.py:538
  29.7 21.2 %all-to-all-start.1 = ((bf16[8,64,256]{2,1,0:T(8,128)(2,1)}), bf16[8,64,256]{2,1,0:T(8,128)(2,1)S(1)}, u32[]{:S(2)}, u32[]{:S(2)}) async-start(bf16[8,64,256]{2,1,0:T(8,128)(2,1)} %get-tuple-element.27), calls=%async_computation.1 | async-start | bytes 524288 | tf_op jit(solution)/shard_map/all_to_all | solution.py:500
Sparse Core Ops, SparseCore 0:
  29.9 38.5 all-gather.2
